TPU v7x, 256 devices: a whole 4x4x8 slice. The times are simulated.
256 devices in a mesh: row: 16 (over z_hi, x, core), col: 16 (over z_lo, y).
Axes of the slice: x: 4, y: 4, z: 8 (z_hi: 2, z_lo: 4; z = z_hi * 4 + z_lo), core: 2. Of those that a mesh axis runs over, the one named last changes fastest.
Arguments:
- ao_ints: bfloat16 [5120, 15360], P(('row', 'col')), may hold values from -6 to 6
- vir_coef: bfloat16 [5120, 128], P(('row', 'col')), may hold values from -0.3125 to 0.3125
- naf_vectors: bfloat16 [15360, 7168], P('row', 'col'), may hold values from -0.046875 to 0.046875
Outputs:
- gram: float32 [15360, 15360], P('row', 'col')
- naf_ints: float32 [128, 7168], P('row', 'col')
All inputs are finite; a program needn't handle non-finite values.
Results may differ from a plain program's by a relative error of at most 0.004.
Values may be sent and summed in bfloat16 or wider, within the bound.
A program may use at most 64 MiB of HBM per device.

v0:
```python
import jax
import jax.numpy as jnp
from jax import lax
from jax.sharding import PartitionSpec as P


def contract_first(lhs, rhs):
    return lax.dot_general(lhs, rhs, (((0,), (0,)), ((), ())), preferred_element_type=jnp.float32)


def contract_second(lhs, rhs):
    return lax.dot_general(lhs, rhs, (((1,), (1,)), ((), ())), preferred_element_type=jnp.float32)


def shards(ao_ints, vir_coef, naf_vectors):
    n_row = lax.axis_size("row")
    n_col = lax.axis_size("col")
    virtuals = vir_coef.shape[1]
    aux_total = ao_ints.shape[1]
    row_width = aux_total // n_row
    col_width = aux_total // n_col
    row_index = lax.axis_index("row")
    col_index = lax.axis_index("col")
    owned_rows = lax.psum_scatter(
        contract_first(ao_ints, vir_coef), ("row", "col"), scatter_dimension=0, tiled=True
    ).astype(jnp.bfloat16)
    gathered = lax.all_gather(owned_rows, ("row", "col"), axis=0, tiled=True)
    panel_rows = lax.dynamic_slice_in_dim(gathered, row_index * row_width, row_width, 0)
    panel_cols = lax.dynamic_slice_in_dim(gathered, col_index * col_width, col_width, 0)
    tile_sum = contract_second(panel_rows, panel_cols)
    projection = contract_first(panel_rows, naf_vectors)
    naf_ints = lax.psum_scatter(projection, "row", scatter_dimension=0, tiled=True)
    return (tile_sum * (1.0 / virtuals), naf_ints)


def solution(mesh):
    in_specs = (P(("row", "col"), None), P(("row", "col"), None), P("row", "col"))
    out_specs = (P("row", "col"), P("row", "col"))
    return jax.shard_map(shards, mesh=mesh, in_specs=in_specs, out_specs=out_specs, check_vma=False)
```

profile of v0, /device:TPU:1, one launch (start us, length us, event | category | flops | bytes accessed | tf_op | source)
XLA Modules:
  0.0 1556.0 jit_solution(640692633945576781)
XLA Ops:
  7.2 5.5 fusion.9
  12.7 652.8 %fusion = f32[64,128]{1,0:T(8,128)S(1)} fusion(f32[15360,128]{1,0:T(8,128)} %fusion.9), kind=kCustom, calls=%all-reduce-scatter | all-reduce-scatter fusion | flops 2097153 | bytes 7897088
  665.5 1.9 collective-permute-start.15
  667.4 1.9 collective-permute-start
  669.4 1.9 collective-permute-start.1
  671.3 1.9 collective-permute-start.10
  673.2 1.9 collective-permute-start.11
  675.2 24.4 %collective-permute-done.15 = bf16[60,128]{1,0:T(8,128)(2,1)S(1)} collective-permute-done((bf16[60,128]{1,0:T(8,128)(2,1)S(1)}, bf16[60,128]{1,0:T(8,128)(2,1)S(1)}, u32[]{:S(2)}, u32[]{:S(2)}) %collective-permute-start.15) | collective-permute-done | bytes 15392
  701.5 1.9 collective-permute-start.13
  703.4 1.9 collective-permute-start.14
  705.4 1.9 collective-permute-start.2
  707.3 1.9 collective-permute-start.3
  709.3 1.9 collective-permute-start.4
  713.1 20.5 %collective-permute-start.6 = (bf16[64,128]{1,0:T(8,128)(2,1)S(1)}, bf16[64,128]{1,0:T(8,128)(2,1)S(1)}, u32[]{:S(2)}, u32[]{:S(2)}) collective-permute-start(bf16[64,128]{1,0:T(8,128)(2,1)S(1)} %convert.30), channel_id=1, source_target_pairs={{0,7},{1,8},{2,9},{3,10},{4,11},{5,12},{6,13},{7,14},{8,15},{9,16}... | collective-permute-start | bytes 49160
  733.6 16.2 %collective-permute-start.7 = (bf16[64,128]{1,0:T(8,128)(2,1)S(1)}, bf16[64,128]{1,0:T(8,128)(2,1)S(1)}, u32[]{:S(2)}, u32[]{:S(2)}) collective-permute-start(bf16[64,128]{1,0:T(8,128)(2,1)S(1)} %convert.30), channel_id=1, source_target_pairs={{0,8},{1,9},{2,10},{3,11},{4,12},{5,13},{6,14},{7,15},{8,16},{9,17... | collective-permute-start | bytes 49160
  749.8 3.4 collective-permute-start.8
  753.2 4.3 collective-permute-start.9
  757.6 3.1 collective-permute-done.9
  760.7 2.7 concatenate
  764.1 703.4 %all-gather.3.cloned.1.call-done = bf16[256,60,128]{2,1,0:T(8,128)(2,1)} async-done(((bf16[1,60,128]{2,1,0:T(8,128)(2,1)}), bf16[256,60,128]{2,1,0:T(8,128)(2,1)}) %all-gather.3.cloned.1.call-update) | async-done | bytes 3932176 | tf_op jit(solution)/shard_map/all_gather | solution.py:27
  1467.5 6.7 reshape.5
  1474.2 2.1 fusion.2
  1476.3 3.7 convolution_multiply_fusion
  1480.0 69.2 %reduce-scatter.4.cloned.1.call-done = f32[8,448]{1,0:T(8,128)} async-done(((f32[128,448]{1,0:T(8,128)}), f32[8,448]{1,0:T(8,128)}) %reduce-scatter.4.cloned.1.call-update) | async-done | bytes 14352 | tf_op jit(solution)/shard_map/reduce_scatter | solution.py:32
  (25 shorter events, 4.6 us)
Async XLA Ops:
  7.2 1467.0 %copy-start = (bf16[960,448]{0,1:T(8,128)(2,1)S(1)}, bf16[960,448]{0,1:T(8,128)(2,1)}, u32[]{:S(2)}) copy-start(bf16[960,448]{0,1:T(8,128)(2,1)} %param.5) | copy-start | bytes 2580484
  7.2 1460.3 %all-gather.3.cloned.1.call-start = ((), (), s32[]{:S(2)}) async-start(), calls=%async_computation.2 | async-start | bytes 4210688 | tf_op jit(solution)/shard_map/all_gather | solution.py:27
  665.5 34.1 %collective-permute-start.15 = (bf16[60,128]{1,0:T(8,128)(2,1)S(1)}, bf16[60,128]{1,0:T(8,128)(2,1)S(1)}, u32[]{:S(2)}, u32[]{:S(2)}) collective-permute-start(bf16[60,128]{1,0:T(8,128)(2,1)S(1)} %slice), channel_id=1, source_target_pairs={{0,16},{1,17},{2,18},{3,19},{4,20},{5,21},{6,22},{7,23},{8,24},{9,... | collective-permute-start | bytes 46088
  667.4 34.0 %collective-permute-start = (bf16[64,128]{1,0:T(8,128)(2,1)S(1)}, bf16[64,128]{1,0:T(8,128)(2,1)S(1)}, u32[]{:S(2)}, u32[]{:S(2)}) collective-permute-start(bf16[64,128]{1,0:T(8,128)(2,1)S(1)} %convert.30), channel_id=1, source_target_pairs={{0,1},{1,2},{2,3},{3,4},{4,5},{5,6},{6,7},{7,8},{8,9},{9,10},{10,1... | collective-permute-start | bytes 49160
  669.4 34.1 %collective-permute-start.1 = (bf16[64,128]{1,0:T(8,128)(2,1)S(1)}, bf16[64,128]{1,0:T(8,128)(2,1)S(1)}, u32[]{:S(2)}, u32[]{:S(2)}) collective-permute-start(bf16[64,128]{1,0:T(8,128)(2,1)S(1)} %convert.30), channel_id=1, source_target_pairs={{0,2},{1,3},{2,4},{3,5},{4,6},{5,7},{6,8},{7,9},{8,10},{9,11},{10,... | collective-permute-start | bytes 49160
  671.3 34.1 %collective-permute-start.10 = (bf16[64,128]{1,0:T(8,128)(2,1)S(1)}, bf16[64,128]{1,0:T(8,128)(2,1)S(1)}, u32[]{:S(2)}, u32[]{:S(2)}) collective-permute-start(bf16[64,128]{1,0:T(8,128)(2,1)S(1)} %convert.30), channel_id=1, source_target_pairs={{0,11},{1,12},{2,13},{3,14},{4,15},{5,16},{6,17},{7,18},{8,19},{9,... | collective-permute-start | bytes 49160
  673.2 34.1 %collective-permute-start.11 = (bf16[64,128]{1,0:T(8,128)(2,1)S(1)}, bf16[64,128]{1,0:T(8,128)(2,1)S(1)}, u32[]{:S(2)}, u32[]{:S(2)}) collective-permute-start(bf16[64,128]{1,0:T(8,128)(2,1)S(1)} %convert.30), channel_id=1, source_target_pairs={{0,12},{1,13},{2,14},{3,15},{4,16},{5,17},{6,18},{7,19},{8,20},{9,... | collective-permute-start | bytes 49160
  699.6 9.7 collective-permute-start.12
  701.5 9.7 collective-permute-start.13
  703.4 9.7 collective-permute-start.14
  705.4 28.2 %collective-permute-start.2 = (bf16[64,128]{1,0:T(8,128)(2,1)S(1)}, bf16[64,128]{1,0:T(8,128)(2,1)S(1)}, u32[]{:S(2)}, u32[]{:S(2)}) collective-permute-start(bf16[64,128]{1,0:T(8,128)(2,1)S(1)} %convert.30), channel_id=1, source_target_pairs={{0,3},{1,4},{2,5},{3,6},{4,7},{5,8},{6,9},{7,10},{8,11},{9,12},{10... | collective-permute-start | bytes 49160
  707.3 42.5 %collective-permute-start.3 = (bf16[64,128]{1,0:T(8,128)(2,1)S(1)}, bf16[64,128]{1,0:T(8,128)(2,1)S(1)}, u32[]{:S(2)}, u32[]{:S(2)}) collective-permute-start(bf16[64,128]{1,0:T(8,128)(2,1)S(1)} %convert.30), channel_id=1, source_target_pairs={{0,4},{1,5},{2,6},{3,7},{4,8},{5,9},{6,10},{7,11},{8,12},{9,13},{1... | collective-permute-start | bytes 49160
  709.3 44.0 %collective-permute-start.4 = (bf16[64,128]{1,0:T(8,128)(2,1)S(1)}, bf16[64,128]{1,0:T(8,128)(2,1)S(1)}, u32[]{:S(2)}, u32[]{:S(2)}) collective-permute-start(bf16[64,128]{1,0:T(8,128)(2,1)S(1)} %convert.30), channel_id=1, source_target_pairs={{0,5},{1,6},{2,7},{3,8},{4,9},{5,10},{6,11},{7,12},{8,13},{9,14},{... | collective-permute-start | bytes 49160
  711.2 46.3 %collective-permute-start.5 = (bf16[64,128]{1,0:T(8,128)(2,1)S(1)}, bf16[64,128]{1,0:T(8,128)(2,1)S(1)}, u32[]{:S(2)}, u32[]{:S(2)}) collective-permute-start(bf16[64,128]{1,0:T(8,128)(2,1)S(1)} %convert.30), channel_id=1, source_target_pairs={{0,6},{1,7},{2,8},{3,9},{4,10},{5,11},{6,12},{7,13},{8,14},{9,15},... | collective-permute-start | bytes 49160
  713.1 44.4 %collective-permute-start.6 = (bf16[64,128]{1,0:T(8,128)(2,1)S(1)}, bf16[64,128]{1,0:T(8,128)(2,1)S(1)}, u32[]{:S(2)}, u32[]{:S(2)}) collective-permute-start(bf16[64,128]{1,0:T(8,128)(2,1)S(1)} %convert.30), channel_id=1, source_target_pairs={{0,7},{1,8},{2,9},{3,10},{4,11},{5,12},{6,13},{7,14},{8,15},{9,16}... | collective-permute-start | bytes 49160
  733.6 23.9 %collective-permute-start.7 = (bf16[64,128]{1,0:T(8,128)(2,1)S(1)}, bf16[64,128]{1,0:T(8,128)(2,1)S(1)}, u32[]{:S(2)}, u32[]{:S(2)}) collective-permute-start(bf16[64,128]{1,0:T(8,128)(2,1)S(1)} %convert.30), channel_id=1, source_target_pairs={{0,8},{1,9},{2,10},{3,11},{4,12},{5,13},{6,14},{7,15},{8,16},{9,17... | collective-permute-start | bytes 49160
  749.8 7.8 collective-permute-start.8
  753.2 7.5 collective-permute-start.9
  764.0 785.1 %reduce-scatter.4.cloned.1.call-start = ((), (), s32[]{:S(2)}) async-start(), calls=%async_computation.1 | async-start | bytes 278528 | tf_op jit(solution)/shard_map/reduce_scatter | solution.py:32
Sparse Core Ops, SparseCore 0:
  764.2 703.2 all-gather.2
  1476.4 72.6 reduce-scatter.3
where the time goes:
time: 1560 us
  waiting for transfers between devices  800 us (51%)
  blocking collectives  653 us (42%)
  starting transfers between devices  67.4 us (4%)
    all_gather x1, waiting for transfers between devices, shards(): gathered = lax.all_gather(owned_rows, ('row', 'col'), axis=0, tiled=True)  703 us
    unnamed x1, blocking collectives  653 us
    reduce_scatter x1, waiting for transfers between devices, shards(): lax.psum_scatter(projection, 'row', scatter_dimension=0, tiled=True)  69.2 us
    unnamed x16, starting transfers between devices  67.4 us
  transfers between devices with their start and end apart: 18, of which 4 were waited for; matrix products, arithmetic and copies ran while one was open for 0% of the time, Pallas kernels for 0%

commit v1 on v0

v1 whole, which is shorter than its diff:
```python
import jax
import jax.numpy as jnp
from jax import lax
from jax.experimental import pallas as pl
from jax.experimental.pallas import tpu as pltpu
from jax.sharding import PartitionSpec as P

MESH = pl.DeviceIdType.MESH
F32 = jnp.float32
BF16 = jnp.bfloat16

LINE = 8
PLANE = 32
OWNERS = 30
UNIT = 64
PANEL = 15


def contract_first(lhs, rhs):
    return lax.dot_general(lhs, rhs, (((0,), (0,)), ((), ())), preferred_element_type=F32)


def contract_second(lhs, rhs):
    return lax.dot_general(lhs, rhs, (((1,), (1,)), ((), ())), preferred_element_type=F32)


def kernel(
    ao_hbm, vir_ref, naf_hbm, gram_ref, naf_ref,
    ao, naf, stage, raw, part, terms, units, rowp, colp, proj, projs,
    load_sem, raw_send, raw_recv, term_send, term_recv, unit_send, unit_recv,
    row_send, col_send, row_recv, col_recv, proj_send, proj_recv,
):
    r = lax.axis_index("row")
    c = lax.axis_index("col")
    zh, i, zl, y = r // 8, r % 8, c // 4, c % 4
    z = 4 * zh + zl
    base = (15 * y + 1) // 2
    owner = base + i
    owns = i < 8 - y % 2

    def term_copy(other):
        return pltpu.make_async_remote_copy(
            src_ref=part.at[other], dst_ref=terms.at[z],
            send_sem=term_send.at[other], recv_sem=term_recv,
            device_id=(8 * (other // 4) + i, 4 * (other % 4) + y), device_id_type=MESH,
        )

    def unit_copy(step):
        if step < 3:
            to_zh, to_zl = zh, (zl + step + 1) % 4
        else:
            to_zh, to_zl = 1 - zh, z // 2
        return pltpu.make_async_remote_copy(
            src_ref=units.at[z], dst_ref=units.at[z],
            send_sem=unit_send.at[step], recv_sem=unit_recv,
            device_id=(8 * to_zh + i, 4 * to_zl + y), device_id_type=MESH,
        )

    def row_target(step):
        unit = 4 * zh + step // 4
        place = 2 * owner + unit % 2
        return unit, 4 * (unit // 2) + place // 15, place % 15, 4 * zl + (y + step) % 4

    def row_copy(step):
        unit, panel, slot, col = row_target(step)
        return pltpu.make_async_remote_copy(
            src_ref=units.at[unit], dst_ref=rowp.at[slot],
            send_sem=row_send.at[step], recv_sem=row_recv,
            device_id=(panel, col), device_id_type=MESH,
        )

    def col_target(step):
        unit = 2 * zl + step // 8
        place = 2 * owner + unit % 2
        return unit, 4 * zl + place // 15, place % 15, 8 * zh + (i + step) % 8

    def col_copy(step):
        unit, panel, slot, row = col_target(step)
        return pltpu.make_async_remote_copy(
            src_ref=units.at[unit], dst_ref=colp.at[slot],
            send_sem=col_send.at[step], recv_sem=col_recv,
            device_id=(row, panel), device_id_type=MESH,
        )

    def proj_copy(other):
        return pltpu.make_async_remote_copy(
            src_ref=proj.at[other], dst_ref=projs.at[r],
            send_sem=proj_send.at[other], recv_sem=proj_recv,
            device_id=(other, c), device_id_type=MESH,
        )

    load_ao = pltpu.make_async_copy(ao_hbm, ao, load_sem.at[0])
    load_naf = pltpu.make_async_copy(naf_hbm, naf, load_sem.at[1])
    load_ao.start()
    load_naf.start()

    barrier = pltpu.get_barrier_semaphore()

    def greet(row, col):
        pl.semaphore_signal(barrier, inc=1, device_id=(row, col), device_id_type=MESH)

    @pl.loop(1, PLANE)
    def _(step):
        other = (8 * y + i + step) % PLANE
        greet(8 * zh + other % 8, 4 * zl + other // 8)

    @pl.loop(1, LINE)
    def _(step):
        other = (z + step) % LINE
        greet(8 * (other // 4) + i, 4 * (other % 4) + y)

    @pl.loop(1, 8)
    def _(step):
        greet(8 * (1 - zh) + (i + step) % 8, c)

    pl.semaphore_wait(barrier, PLANE - 1 + LINE - 1 + 7)

    load_ao.wait()
    tail = vir_ref[16:20, :].astype(F32)
    vir_tail = jnp.concatenate([tail, tail, tail, tail], axis=0).astype(BF16)
    vir_main = vir_ref[0:16, :]

    def raw_copy(dest):
        dest_y = (2 * dest) // 15
        dest_i = dest - (15 * dest_y + 1) // 2
        return pltpu.make_async_remote_copy(
            src_ref=stage.at[dest], dst_ref=raw.at[8 * y + i],
            send_sem=raw_send.at[dest], recv_sem=raw_recv,
            device_id=(8 * zh + dest_i, 4 * zl + dest_y), device_id_type=MESH,
        )

    @pl.loop(0, OWNERS)
    def _(step):
        dest = (base + i + step) % OWNERS
        tails = []
        for quarter in range(4):
            lanes = pl.ds(pl.multiple_of(128 * (30 * quarter + dest), 128), 128)
            stage[dest, 16 * quarter : 16 * quarter + 16, :] = ao[0:16, lanes]
            tails.append(ao[16:20, lanes].astype(F32))
        stage[dest, 64:80, :] = jnp.concatenate(tails, axis=0).astype(BF16)
        stage[dest, 80:96, :] = vir_main
        stage[dest, 96:112, :] = vir_tail
        mine = jnp.logical_and(owns, dest == owner)

        @pl.when(mine)
        def _():
            pltpu.make_async_copy(stage.at[dest], raw.at[8 * y + i], raw_recv).start()

        @pl.when(jnp.logical_not(mine))
        def _():
            raw_copy(dest).start()

    @pl.when(owns)
    def _():
        pltpu.make_async_copy(raw, raw, raw_recv).wait()
        coeff = raw[:, 80:96, :].reshape(512, 128)
        coeff_tail = raw[:, 96:112, :].reshape(512, 128)
        ints_tail = raw[:, 64:80, :].reshape(512, 128)
        which = (lax.broadcasted_iota(jnp.int32, (512, 128), 0) // 4) % 4
        for quarter in range(4):
            ints = raw[:, 16 * quarter : 16 * quarter + 16, :].reshape(512, 128)
            picked = jnp.where(which == quarter, coeff_tail.astype(F32), 0.0).astype(BF16)
            half = contract_first(ints, coeff) + contract_first(ints_tail, picked)
            part[2 * quarter, :, :] = half[0:UNIT, :]
            part[2 * quarter + 1, :, :] = half[UNIT:, :]

        pltpu.make_async_copy(part.at[z], terms.at[z], term_recv).start()

        @pl.loop(1, LINE)
        def _(step):
            other = (z + step) % LINE
            term_copy(other).start()

        pltpu.make_async_copy(terms, terms, term_recv).wait()
        total = terms[0, :, :]
        for s in range(1, LINE):
            total = total + terms[s, :, :]
        units[z, :, :] = total.astype(BF16)

        for step in range(4):
            unit_copy(step).start()
        crossed = zl // 2 != zh

        @pl.when(crossed)
        def _():
            pltpu.make_async_copy(units.at[pl.ds(0, 5)], units.at[pl.ds(0, 5)], unit_recv).wait()

        @pl.when(jnp.logical_not(crossed))
        def _():
            pltpu.make_async_copy(units.at[pl.ds(0, 3)], units.at[pl.ds(0, 3)], unit_recv).wait()

        @pl.loop(0, 16)
        def _(step):
            unit, panel, slot, col = row_target(step)
            mine = jnp.logical_and(panel == r, col == c)

            @pl.when(mine)
            def _():
                pltpu.make_async_copy(units.at[unit], rowp.at[slot], row_recv).start()

            @pl.when(jnp.logical_not(mine))
            def _():
                row_copy(step).start()

        @pl.loop(0, 16)
        def _(step):
            unit, panel, slot, row = col_target(step)
            mine = jnp.logical_and(panel == c, row == r)

            @pl.when(mine)
            def _():
                pltpu.make_async_copy(units.at[unit], colp.at[slot], col_recv).start()

            @pl.when(jnp.logical_not(mine))
            def _():
                col_copy(step).start()

    load_naf.wait()
    pltpu.make_async_copy(rowp, rowp, row_recv).wait()
    rows = rowp[...].reshape(PANEL * UNIT, 128)
    proj[...] = contract_first(rows, naf[...]).reshape(16, 8, naf.shape[1])
    pltpu.make_async_copy(proj.at[r], projs.at[r], proj_recv).start()

    @pl.loop(1, 16)
    def _(step):
        proj_copy((r + step) % 16).start()

    pltpu.make_async_copy(colp, colp, col_recv).wait()
    cols = colp[...].reshape(PANEL * UNIT, 128)
    for part_of in range(5):
        block = rowp[3 * part_of : 3 * part_of + 3, :, :].reshape(3 * UNIT, 128)
        gram_ref[3 * UNIT * part_of : 3 * UNIT * (part_of + 1), :] = contract_second(block, cols) * (1.0 / 128)

    pltpu.make_async_copy(projs, projs, proj_recv).wait()
    total = projs[0, :, :]
    for s in range(1, 16):
        total = total + projs[s, :, :]
    naf_ref[...] = total

    @pl.loop(0, OWNERS)
    def _(dest):
        @pl.when(jnp.logical_not(jnp.logical_and(owns, dest == owner)))
        def _():
            raw_copy(dest).wait_send()

    @pl.when(owns)
    def _():
        @pl.loop(1, LINE)
        def _(step):
            term_copy((z + step) % LINE).wait_send()

        for step in range(4):
            unit_copy(step).wait_send()

        @pl.loop(0, 16)
        def _(step):
            unit, panel, slot, col = row_target(step)

            @pl.when(jnp.logical_not(jnp.logical_and(panel == r, col == c)))
            def _():
                row_copy(step).wait_send()

        @pl.loop(0, 16)
        def _(step):
            unit, panel, slot, row = col_target(step)

            @pl.when(jnp.logical_not(jnp.logical_and(panel == c, row == r)))
            def _():
                col_copy(step).wait_send()

    @pl.loop(1, 16)
    def _(step):
        proj_copy((r + step) % 16).wait_send()


def shards(ao_ints, vir_coef, naf_vectors):
    dma = pltpu.SemaphoreType.DMA
    return pl.pallas_call(
        kernel,
        out_shape=(
            jax.ShapeDtypeStruct((960, 960), F32),
            jax.ShapeDtypeStruct((8, 448), F32),
        ),
        in_specs=[
            pl.BlockSpec(memory_space=pl.ANY),
            pl.BlockSpec(memory_space=pltpu.VMEM),
            pl.BlockSpec(memory_space=pl.ANY),
        ],
        out_specs=(
            pl.BlockSpec(memory_space=pltpu.VMEM),
            pl.BlockSpec(memory_space=pltpu.VMEM),
        ),
        scratch_shapes=[
            pltpu.VMEM((20, 15360), BF16),
            pltpu.VMEM((960, 448), BF16),
            pltpu.VMEM((OWNERS, 112, 128), BF16),
            pltpu.VMEM((PLANE, 112, 128), BF16),
            pltpu.VMEM((LINE, UNIT, 128), F32),
            pltpu.VMEM((LINE, UNIT, 128), F32),
            pltpu.VMEM((LINE, UNIT, 128), BF16),
            pltpu.VMEM((PANEL, UNIT, 128), BF16),
            pltpu.VMEM((PANEL, UNIT, 128), BF16),
            pltpu.VMEM((16, 8, 448), F32),
            pltpu.VMEM((16, 8, 448), F32),
            dma((2,)), dma((OWNERS,)), dma, dma((LINE,)), dma, dma((4,)), dma,
            dma((16,)), dma((16,)), dma, dma, dma((16,)), dma,
        ],
        compiler_params=pltpu.CompilerParams(
            collective_id=0, has_side_effects=True, vmem_limit_bytes=40 * 1024 * 1024
        ),
        name="gram_and_projection",
    )(ao_ints, vir_coef, naf_vectors)


def solution(mesh):
    in_specs = (P(("row", "col"), None), P(("row", "col"), None), P("row", "col"))
    out_specs = (P("row", "col"), P("row", "col"))
    return jax.shard_map(shards, mesh=mesh, in_specs=in_specs, out_specs=out_specs, check_vma=False)
```

time: 1560 us -> 65.1 us (0.04)
  waiting for transfers between devices: 800 us -> 0 us
  blocking collectives: 653 us -> 0 us
  starting transfers between devices: 67.4 us -> 0 us
  Pallas kernels: 0 us -> 58.3 us
    all_gather x1 -> x0, waiting for transfers between devices: 703 us -> none  [shards(): gathered = lax.all_gather(owned_rows, ('row', 'col'), axis=0, tiled=True)]
    unnamed x1 -> x0, blocking collectives: 653 us -> none
    reduce_scatter x1 -> x0, waiting for transfers between devices: 69.2 us -> none  [shards(): lax.psum_scatter(projection, 'row', scatter_dimension=0, tiled=True)]
    unnamed x16 -> x0, starting transfers between devices: 67.4 us -> none
    pallas_call x0 -> x1, Pallas kernels: none -> 58.3 us  [shards(): pl.pallas_call(kernel, out_shape=(jax.ShapeDtypeStruct((960, 960), F32),...]
    unnamed x18 -> x0, waiting for transfers between devices: 27.6 us -> none
  transfers between devices with their start and end apart: 18 -> 0, of which waited for: 4 -> 0; matrix products, arithmetic and copies ran while one was open for 0% -> 0% of each run, Pallas kernels for 0% -> 0%
where the time goes in v1:
time: 65.1 us; the launch traced here: 64.9 us
  Pallas kernels  58.3 us (90%)
  local copies, waits for them, and re-layouts  5.99 us (9%)
  between operations  0.66 us (1%)
    pallas_call x1, Pallas kernels, shards(): pl.pallas_call(kernel, out_shape=(jax.ShapeDtypeStruct((960, 960), F32),...  58.3 us
    unnamed x7, local copies, waits for them, and re-layouts  5.99 us

profile of v1, /device:TPU:1, one launch (start us, length us, event | category | flops | bytes accessed | tf_op | source)
XLA Modules:
  0.0 64.9 jit_solution(13273113206385306222)
XLA Ops:
  0.6 1.7 %copy.5.naf_hbm = bf16[960,448]{1,0:T(8,128)(2,1)S(1)} copy(bf16[960,448]{0,1:T(8,128)(2,1)} %param.5) | data formatting | bytes 1720320 | tf_op args[2]
  2.3 0.0 copy-start
  2.3 1.1 %copy-done = bf16[20,15360]{1,0:T(8,128)(2,1)S(1)} copy-done((bf16[20,15360]{1,0:T(8,128)(2,1)S(1)}, bf16[20,15360]{1,0:T(8,128)(2,1)}, u32[]{:S(2)}) %copy-start) | copy-done | bytes 614424
  3.4 0.0 copy-start.1
  3.4 0.7 %copy-done.1 = bf16[20,128]{1,0:T(8,128)(2,1)S(1)} copy-done((bf16[20,128]{1,0:T(8,128)(2,1)S(1)}, bf16[20,128]{1,0:T(8,128)(2,1)}, u32[]{:S(2)}) %copy-start.1) | copy-done | bytes 5144
  4.1 58.3 %gram_and_projection.1 = (f32[960,960]{1,0:T(8,128)S(1)}, f32[8,448]{1,0:T(8,128)S(1)}) custom-call(bf16[20,15360]{1,0:T(8,128)(2,1)S(1)} %copy-done, bf16[20,128]{1,0:T(8,128)(2,1)S(1)} %copy-done.1, bf16[960,448]{1,0:T(8,128)(2,1)S(1)} %copy.5.naf_hbm), custom_call_target="tpu_custom_call" | custom-call | tf_op jit(solution)/shard_map/gram_and_projection/pallas_call | solution.py:278
  62.4 1.9 %copy.8 = f32[960,960]{1,0:T(8,128)} copy(f32[960,960]{1,0:T(8,128)S(1)} %get-tuple-element.4) | data formatting | bytes 7372800
  64.3 0.6 copy.9
Async XLA Ops:
  2.3 1.1 %copy-start = (bf16[20,15360]{1,0:T(8,128)(2,1)S(1)}, bf16[20,15360]{1,0:T(8,128)(2,1)}, u32[]{:S(2)}) copy-start(bf16[20,15360]{1,0:T(8,128)(2,1)} %ao_hbm.1) | copy-start | bytes 1843204
  3.4 0.7 %copy-start.1 = (bf16[20,128]{1,0:T(8,128)(2,1)S(1)}, bf16[20,128]{1,0:T(8,128)(2,1)}, u32[]{:S(2)}) copy-start(bf16[20,128]{1,0:T(8,128)(2,1)} %vir_ref.1) | copy-start | bytes 15364

commit v2 on v0

v2 whole, which is shorter than its diff:
```python
import jax
import jax.numpy as jnp
from jax import lax
from jax.experimental import pallas as pl
from jax.experimental.pallas import tpu as pltpu
from jax.sharding import PartitionSpec as P

MESH = pl.DeviceIdType.MESH
F32 = jnp.float32
BF16 = jnp.bfloat16

LINE = 8
PLANE = 32
UNIT = 64
PANEL = 15
SHIFTS = (2, 1, 3, 0)
SPANS = ((0, 32), (32, 48), (48, 64), (64, 80))


def contract_first(lhs, rhs):
    return lax.dot_general(lhs, rhs, (((0,), (0,)), ((), ())), preferred_element_type=F32)


def contract_second(lhs, rhs):
    return lax.dot_general(lhs, rhs, (((1,), (1,)), ((), ())), preferred_element_type=F32)


def owner_of(x, y, core):
    return (15 * y + 1) // 2 + 2 * x + core, 2 * x + core < 8 - y % 2


def kernel(
    ao_hbm, vir_hbm, naf_hbm, gram_ref, naf_ref,
    ao, vir, naf, stage, raw, vsend, coeffs, part, terms, units, rowp, colp, proj, projs,
    load_sem, vir_send, vir_recv, pass_send, pass_recv, raw_send, raw_recv, self_sem, term_send, term_recv,
    unit_send, unit_recv, row_send, col_send, row_recv, col_recv, proj_send, proj_recv,
):
    r = lax.axis_index("row")
    c = lax.axis_index("col")
    zh, x, core, zl, y = r // 8, (r // 2) % 4, r % 2, c // 4, c % 4
    i = 2 * x + core
    z = 4 * zh + zl
    chip = 4 * y + x
    place = 16 * core + chip
    owner, owns = owner_of(x, y, core)

    load_ao = pltpu.make_async_copy(ao_hbm, ao, load_sem.at[0])
    load_naf = pltpu.make_async_copy(naf_hbm, naf, load_sem.at[1])
    load_vir = pltpu.make_async_copy(vir_hbm, vir, load_sem.at[2])
    load_vir.start()
    load_ao.start()
    load_naf.start()

    barrier = pltpu.get_barrier_semaphore()

    def greet(row, col):
        pl.semaphore_signal(barrier, inc=1, device_id=(row, col), device_id_type=MESH)

    def in_plane(where):
        return 8 * zh + 2 * (where % 4) + where // 16, 4 * zl + (where // 4) % 4

    def in_line(where):
        return 8 * (where // 4) + i, 4 * (where % 4) + y

    @pl.loop(1, PLANE)
    def _(step):
        greet(*in_plane((place + step) % PLANE))

    @pl.loop(1, LINE)
    def _(step):
        greet(*in_line((z + step) % LINE))

    @pl.loop(1, 8)
    def _(step):
        greet(8 * (1 - zh) + (i + step) % 8, c)

    def vir_copy(other):
        return pltpu.make_async_remote_copy(
            src_ref=vsend, dst_ref=coeffs.at[core, chip],
            send_sem=vir_send, recv_sem=vir_recv,
            device_id=in_plane(16 * core + other), device_id_type=MESH,
        )

    pass_copy = pltpu.make_async_remote_copy(
        src_ref=coeffs.at[core], dst_ref=coeffs.at[core],
        send_sem=pass_send, recv_sem=pass_recv,
        device_id=(r + 1 - 2 * core, c), device_id_type=MESH,
    )

    def raw_copy(dest, turn):
        first, last = SPANS[turn]
        return pltpu.make_async_remote_copy(
            src_ref=stage.at[dest, first:last], dst_ref=raw.at[place, first:last],
            send_sem=raw_send.at[turn], recv_sem=raw_recv.at[turn],
            device_id=in_plane(dest), device_id_type=MESH,
        )

    def term_copy(other, turn):
        return pltpu.make_async_remote_copy(
            src_ref=part.at[other], dst_ref=terms.at[z],
            send_sem=term_send, recv_sem=term_recv,
            device_id=in_line(other), device_id_type=MESH,
        )

    def unit_copy(step):
        if step < 3:
            other = 4 * zh + (zl + step + 1) % 4
        else:
            other = 4 * (1 - zh) + z // 2
        return pltpu.make_async_remote_copy(
            src_ref=units.at[z], dst_ref=units.at[z],
            send_sem=unit_send.at[step], recv_sem=unit_recv.at[z],
            device_id=in_line(other), device_id_type=MESH,
        )

    def await_unit(unit):
        pltpu.make_async_copy(units.at[unit], units.at[unit], unit_recv.at[unit]).wait()

    def row_target(step):
        unit = 4 * zh + (zl + step // 4) % 4
        spot = 2 * owner + unit % 2
        return unit, 4 * (unit // 2) + spot // 15, spot % 15, 4 * zl + (y + step) % 4

    def row_copy(step):
        unit, panel, slot, col = row_target(step)
        return pltpu.make_async_remote_copy(
            src_ref=units.at[unit], dst_ref=rowp.at[slot],
            send_sem=row_send.at[step], recv_sem=row_recv,
            device_id=(panel, col), device_id_type=MESH,
        )

    def row_here(step):
        unit, panel, slot, col = row_target(step)
        return jnp.logical_and(panel == r, col == c)

    def col_target(step):
        unit = 2 * zl + step // 8
        spot = 2 * owner + unit % 2
        return unit, 4 * zl + spot // 15, spot % 15, 8 * zh + (i + step) % 8

    def col_copy(step):
        unit, panel, slot, row = col_target(step)
        return pltpu.make_async_remote_copy(
            src_ref=units.at[unit], dst_ref=colp.at[slot],
            send_sem=col_send.at[step], recv_sem=col_recv,
            device_id=(row, panel), device_id_type=MESH,
        )

    def col_here(step):
        unit, panel, slot, row = col_target(step)
        return jnp.logical_and(panel == c, row == r)

    def proj_copy(other):
        return pltpu.make_async_remote_copy(
            src_ref=proj.at[other], dst_ref=projs.at[r],
            send_sem=proj_send, recv_sem=proj_recv,
            device_id=(other, c), device_id_type=MESH,
        )

    def wait_bytes(ref, sem):
        pltpu.make_async_copy(ref, ref, sem).wait()

    load_vir.wait()
    tail = vir[16:20, :].astype(F32)
    vsend[0:16, :] = vir[0:16, :]
    vsend[16:32, :] = jnp.concatenate([tail, tail, tail, tail], axis=0).astype(BF16)
    coeffs[core, chip, :, :] = vsend[...]
    load_ao.wait()
    turns = []
    for quarter in range(4):
        ahead = (quarter + 4 - z // 2) % 4
        turns.append(jnp.where(ahead == 0, 3, jnp.where(ahead == 1, 1, jnp.where(ahead == 2, 0, 2))))
    for dest in range(PLANE):
        theirs, has = owner_of(dest % 4, (dest // 4) % 4, dest // 16)
        if not has:
            continue
        tails = []
        for quarter in range(4):
            lanes = slice(128 * (30 * quarter + theirs), 128 * (30 * quarter + theirs) + 128)
            stage[dest, pl.ds(pl.multiple_of(16 + 16 * turns[quarter], 16), 16), :] = ao[0:16, lanes]
            tails.append(ao[16:20, lanes].astype(F32))
        stage[dest, 0:16, :] = jnp.concatenate(tails, axis=0).astype(BF16)

    pl.semaphore_wait(barrier, PLANE - 1 + LINE - 1 + 7)

    @pl.loop(1, 16)
    def _(step):
        vir_copy((chip + 7 * step) % 16).start()

    for turn in range(4):
        first, last = SPANS[turn]

        @pl.when(owns)
        def _():
            pltpu.make_async_copy(stage.at[place, first:last], raw.at[place, first:last], self_sem.at[turn]).start()

        @pl.loop(1, PLANE)
        def _(step):
            dest = (place + 7 * step) % PLANE
            _, has = owner_of(dest % 4, (dest // 4) % 4, dest // 16)

            @pl.when(has)
            def _():
                raw_copy(dest, turn).start()

    wait_bytes(coeffs.at[core, pl.ds(0, 15)], vir_recv)
    pass_copy.start()
    pass_copy.wait_recv()

    @pl.when(owns)
    def _():
        coeff = coeffs[:, :, 0:16, :].reshape(512, 128)
        coeff_tail = coeffs[:, :, 16:32, :].reshape(512, 128).astype(F32)
        which = (lax.broadcasted_iota(jnp.int32, (512, 128), 0) // 4) % 4
        for turn in range(4):
            quarter = (z // 2 + SHIFTS[turn]) % 4
            first, last = SPANS[turn]
            wait_bytes(raw.at[place, first:last], self_sem.at[turn])
            wait_bytes(raw.at[pl.ds(0, PLANE - 1), first:last], raw_recv.at[turn])
            ints = raw[:, last - 16 : last, :].reshape(512, 128)
            ints_tail = raw[:, 0:16, :].reshape(512, 128)
            picked = jnp.where(which == quarter, coeff_tail, 0.0).astype(BF16)
            half = contract_first(ints, coeff) + contract_first(ints_tail, picked)
            for unit in range(2):
                part[2 * quarter + unit, :, :] = half[UNIT * unit : UNIT * (unit + 1), :]
                other = 2 * quarter + unit
                if turn < 3:
                    term_copy(other, turn).start()
                else:

                    @pl.when(other != z)
                    def _():
                        term_copy(other, turn).start()

        terms[z, :, :] = part[z, :, :]
        wait_bytes(terms.at[pl.ds(0, LINE - 1)], term_recv)
        total = terms[0, :, :]
        for s in range(1, LINE):
            total = total + terms[s, :, :]
        units[z, :, :] = total.astype(BF16)

        for step in range(4):
            unit_copy(step).start()
        for ahead in range(4):
            if ahead:
                await_unit(4 * zh + (zl + ahead) % 4)

            @pl.loop(4 * ahead, 4 * ahead + 4)
            def _(step):
                unit, panel, slot, col = row_target(step)
                here = row_here(step)

                @pl.when(here)
                def _():
                    pltpu.make_async_copy(units.at[unit], rowp.at[slot], row_recv).start()

                @pl.when(jnp.logical_not(here))
                def _():
                    row_copy(step).start()

    load_naf.wait()
    wait_bytes(rowp, row_recv)
    rows = rowp[...].reshape(PANEL * UNIT, 128)
    share = lax.dot_general(naf[...], rows, (((1,), (0,)), ((), ())), preferred_element_type=F32)
    proj[...] = share.T.reshape(16, 8, naf.shape[0])

    @pl.loop(1, 16)
    def _(step):
        proj_copy((r + step) % 16).start()

    projs[r, :, :] = proj[r, :, :]

    @pl.when(owns)
    def _():
        @pl.when(zl // 2 != zh)
        def _():
            await_unit(2 * zl)
            await_unit(2 * zl + 1)

        @pl.loop(0, 16)
        def _(step):
            unit, panel, slot, row = col_target(step)
            here = col_here(step)

            @pl.when(here)
            def _():
                pltpu.make_async_copy(units.at[unit], colp.at[slot], col_recv).start()

            @pl.when(jnp.logical_not(here))
            def _():
                col_copy(step).start()

    wait_bytes(colp, col_recv)
    cols = colp[...].reshape(PANEL * UNIT, 128)
    for band in range(5):
        block = rowp[3 * band : 3 * band + 3, :, :].reshape(3 * UNIT, 128)
        gram_ref[3 * UNIT * band : 3 * UNIT * (band + 1), :] = contract_second(block, cols) * (1.0 / 128)

    wait_bytes(projs.at[pl.ds(0, 15)], proj_recv)
    total = projs[0, :, :]
    for s in range(1, 16):
        total = total + projs[s, :, :]
    naf_ref[...] = total

    wait_bytes(coeffs.at[core, pl.ds(0, 15)], vir_send)
    pass_copy.wait_send()
    for turn in range(4):
        first, last = SPANS[turn]

        @pl.when(owns)
        def _():
            wait_bytes(stage.at[pl.ds(0, 29), first:last], raw_send.at[turn])

        @pl.when(jnp.logical_not(owns))
        def _():
            wait_bytes(stage.at[pl.ds(0, 30), first:last], raw_send.at[turn])

    @pl.when(owns)
    def _():
        wait_bytes(part.at[pl.ds(0, LINE - 1)], term_send)
        for step in range(4):
            unit_copy(step).wait_send()

        @pl.loop(0, 16)
        def _(step):
            @pl.when(jnp.logical_not(row_here(step)))
            def _():
                row_copy(step).wait_send()

        @pl.loop(0, 16)
        def _(step):
            @pl.when(jnp.logical_not(col_here(step)))
            def _():
                col_copy(step).wait_send()

    wait_bytes(proj.at[pl.ds(0, 15)], proj_send)


def shards(ao_ints, vir_coef, naf_vectors):
    dma = pltpu.SemaphoreType.DMA
    hbm = pl.BlockSpec(memory_space=pltpu.HBM)
    return pl.pallas_call(
        kernel,
        out_shape=(
            jax.ShapeDtypeStruct((960, 960), F32),
            jax.ShapeDtypeStruct((8, 448), F32),
        ),
        in_specs=[hbm, hbm, hbm],
        out_specs=(
            pl.BlockSpec(memory_space=pltpu.VMEM),
            pl.BlockSpec(memory_space=pltpu.VMEM),
        ),
        scratch_shapes=[
            pltpu.VMEM((20, 15360), BF16),
            pltpu.VMEM((20, 128), BF16),
            pltpu.VMEM((448, 960), BF16),
            pltpu.VMEM((PLANE, 80, 128), BF16),
            pltpu.VMEM((PLANE, 80, 128), BF16),
            pltpu.VMEM((32, 128), BF16),
            pltpu.VMEM((2, 16, 32, 128), BF16),
            pltpu.VMEM((LINE, UNIT, 128), F32),
            pltpu.VMEM((LINE, UNIT, 128), F32),
            pltpu.VMEM((LINE, UNIT, 128), BF16),
            pltpu.VMEM((PANEL, UNIT, 128), BF16),
            pltpu.VMEM((PANEL, UNIT, 128), BF16),
            pltpu.VMEM((16, 8, 448), F32),
            pltpu.VMEM((16, 8, 448), F32),
            dma((3,)), dma, dma, dma, dma, dma((4,)), dma((4,)), dma((4,)), dma, dma,
            dma((4,)), dma((LINE,)), dma((16,)), dma((16,)), dma, dma, dma, dma,
        ],
        compiler_params=pltpu.CompilerParams(
            collective_id=0, has_side_effects=True, vmem_limit_bytes=40 * 1024 * 1024
        ),
        name="gram_and_projection",
    )(*(pltpu.with_memory_space_constraint(a, pltpu.HBM) for a in (ao_ints, vir_coef, naf_vectors.T)))


def solution(mesh):
    in_specs = (P(("row", "col"), None), P(("row", "col"), None), P("row", "col"))
    out_specs = (P("row", "col"), P("row", "col"))
    return jax.shard_map(shards, mesh=mesh, in_specs=in_specs, out_specs=out_specs, check_vma=False)
```

time: 1560 us -> 54.9 us (0.04)
  waiting for transfers between devices: 800 us -> 0 us
  blocking collectives: 653 us -> 0 us
  starting transfers between devices: 67.4 us -> 0 us
  Pallas kernels: 0 us -> 51.6 us
    all_gather x1 -> x0, waiting for transfers between devices: 703 us -> none  [shards(): gathered = lax.all_gather(owned_rows, ('row', 'col'), axis=0, tiled=True)]
    unnamed x1 -> x0, blocking collectives: 653 us -> none
    reduce_scatter x1 -> x0, waiting for transfers between devices: 69.2 us -> none  [shards(): lax.psum_scatter(projection, 'row', scatter_dimension=0, tiled=True)]
    unnamed x16 -> x0, starting transfers between devices: 67.4 us -> none
    pallas_call x0 -> x1, Pallas kernels: none -> 51.6 us  [shards(): pl.pallas_call(kernel, out_shape=(jax.ShapeDtypeStruct((960, 960), F32),...]
    unnamed x18 -> x0, waiting for transfers between devices: 27.6 us -> none
  transfers between devices with their start and end apart: 18 -> 0, of which waited for: 4 -> 0; matrix products, arithmetic and copies ran while one was open for 0% -> 0% of each run, Pallas kernels for 0% -> 0%
where the time goes in v2:
time: 54.9 us; the launch traced here: 54.8 us
  Pallas kernels  51.6 us (94%)
  local copies, waits for them, and re-layouts  2.53 us (5%)
  between operations  0.64 us (1%)
    pallas_call x1, Pallas kernels, shards(): pl.pallas_call(kernel, out_shape=(jax.ShapeDtypeStruct((960, 960), F32),...  51.6 us
    unnamed x2, local copies, waits for them, and re-layouts  2.53 us

profile of v2, /device:TPU:1, one launch (start us, length us, event | category | flops | bytes accessed | tf_op | source)
XLA Modules:
  0.0 54.8 jit_solution(1723106321302563449)
XLA Ops:
  0.6 51.6 %gram_and_projection.1 = (f32[960,960]{1,0:T(8,128)S(1)}, f32[8,448]{1,0:T(8,128)S(1)}) custom-call(bf16[20,15360]{1,0:T(8,128)(2,1)} %ao_hbm.1, bf16[20,128]{1,0:T(8,128)(2,1)} %vir_hbm.1, bf16[448,960]{1,0:T(8,128)(2,1)} %bitcast.1), custom_call_target="tpu_custom_call" | custom-call | tf_op jit(solution)/shard_map/gram_and_projection/pallas_call | solution.py:342
  52.3 1.9 %copy.7 = f32[960,960]{1,0:T(8,128)} copy(f32[960,960]{1,0:T(8,128)S(1)} %get-tuple-element.4) | data formatting | bytes 7372800
  54.2 0.6 %copy.8 = f32[8,448]{1,0:T(8,128)} copy(f32[8,448]{1,0:T(8,128)S(1)} %get-tuple-element.5) | data formatting | bytes 28672

commit v3 on v2

v3 whole, which is shorter than its diff:
```python
import jax
import jax.numpy as jnp
from jax import lax
from jax.experimental import pallas as pl
from jax.experimental.pallas import tpu as pltpu
from jax.sharding import PartitionSpec as P

MESH = pl.DeviceIdType.MESH
F32 = jnp.float32
BF16 = jnp.bfloat16

LINE = 8
PLANE = 32
UNIT = 64
PANEL = 15
SHIFTS = (2, 1, 3, 0)
SPANS = ((0, 48), (48, 64), (64, 80))
AWAITS = (0, None, 1, 2)


def contract_first(lhs, rhs):
    return lax.dot_general(lhs, rhs, (((0,), (0,)), ((), ())), preferred_element_type=F32)


def contract_second(lhs, rhs):
    return lax.dot_general(lhs, rhs, (((1,), (1,)), ((), ())), preferred_element_type=F32)


def kernel(
    ao_hbm, vir_hbm, naf_hbm, gram_ref, naf_ref,
    ao, vir, naf, stage, raw, vsend, coeffs, part, terms, unit, rowp, held, colp, proj, pair, sums, projs,
    load_sem, vir_send, vir_recv, pass_send, pass_recv, raw_send, raw_recv, term_send, term_recv,
    row_send, row_recv, hold_send, hold_recv, col_send, col_recv, half_send, half_recv, pair_send, pair_recv, proj_send, proj_recv,
):
    r = lax.axis_index("row")
    c = lax.axis_index("col")
    zh, x, core, zl, y = r // 8, (r // 2) % 4, r % 2, c // 4, c % 4
    i = 2 * x + core
    z = 4 * zh + zl
    chip = 4 * y + x
    place = 16 * core + chip
    spot = 4 * y + zl
    owns = spot < PANEL

    load_ao = pltpu.make_async_copy(ao_hbm, ao, load_sem.at[0])
    load_naf = pltpu.make_async_copy(naf_hbm, naf, load_sem.at[1])
    load_vir = pltpu.make_async_copy(vir_hbm, vir, load_sem.at[2])
    load_vir.start()
    load_ao.start()
    load_naf.start()

    barrier = pltpu.get_barrier_semaphore()

    def greet(row, col):
        pl.semaphore_signal(barrier, inc=1, device_id=(row, col), device_id_type=MESH)

    def in_plane(where):
        return 8 * zh + 2 * (where % 4) + where // 16, 4 * zl + (where // 4) % 4

    def in_line(where):
        return 8 * (where // 4) + i, 4 * (where % 4) + y

    @pl.loop(1, PLANE)
    def _(step):
        greet(*in_plane((place + step) % PLANE))

    @pl.loop(1, LINE)
    def _(step):
        greet(*in_line((z + step) % LINE))

    @pl.loop(1, 8)
    def _(step):
        greet(8 * (1 - zh) + (i + step) % 8, c)

    def vir_copy(other):
        return pltpu.make_async_remote_copy(
            src_ref=vsend, dst_ref=coeffs.at[core, chip],
            send_sem=vir_send, recv_sem=vir_recv,
            device_id=in_plane(16 * core + other), device_id_type=MESH,
        )

    pass_copy = pltpu.make_async_remote_copy(
        src_ref=coeffs.at[core], dst_ref=coeffs.at[core],
        send_sem=pass_send, recv_sem=pass_recv,
        device_id=(r + 1 - 2 * core, c), device_id_type=MESH,
    )

    def raw_copy(dest, turn):
        first, last = SPANS[turn]
        return pltpu.make_async_remote_copy(
            src_ref=stage.at[dest, first:last], dst_ref=raw.at[place, first:last],
            send_sem=raw_send.at[turn], recv_sem=raw_recv.at[turn],
            device_id=in_plane(dest), device_id_type=MESH,
        )

    def term_copy(other):
        return pltpu.make_async_remote_copy(
            src_ref=part.at[other], dst_ref=terms.at[z],
            send_sem=term_send, recv_sem=term_recv,
            device_id=in_line(other), device_id_type=MESH,
        )

    def row_copy(other):
        return pltpu.make_async_remote_copy(
            src_ref=unit, dst_ref=rowp.at[spot],
            send_sem=row_send, recv_sem=row_recv.at[y],
            device_id=(r, other), device_id_type=MESH,
        )

    goal = r // 4
    holds = x // 2 == zl % 2
    at_home = zl == goal
    goal_y = r % 4

    def hold_copy(half):
        return pltpu.make_async_remote_copy(
            src_ref=unit, dst_ref=held.at[zl],
            send_sem=hold_send, recv_sem=hold_recv,
            device_id=(8 * half + i, 4 * goal + y), device_id_type=MESH,
        )

    col_span = pl.ds(4 * y, 4)

    def col_here(other):
        return jnp.logical_and(other == x, jnp.logical_and(goal_y == y, core == y // 2))

    def col_copy(other):
        return pltpu.make_async_remote_copy(
            src_ref=held, dst_ref=colp.at[col_span],
            send_sem=col_send, recv_sem=col_recv,
            device_id=(8 * zh + 2 * other + y // 2, 4 * zl + goal_y), device_id_type=MESH,
        )

    half_span = pl.ds(8 * core, 8)
    half_copy = pltpu.make_async_remote_copy(
        src_ref=colp.at[half_span], dst_ref=colp.at[half_span],
        send_sem=half_send, recv_sem=half_recv,
        device_id=(r + 1 - 2 * core, c), device_id_type=MESH,
    )

    pair_copy = pltpu.make_async_remote_copy(
        src_ref=proj.at[1 - core], dst_ref=pair,
        send_sem=pair_send, recv_sem=pair_recv,
        device_id=(r + 1 - 2 * core, c), device_id_type=MESH,
    )

    def proj_copy(other):
        return pltpu.make_async_remote_copy(
            src_ref=sums.at[other], dst_ref=projs.at[4 * zh + x],
            send_sem=proj_send, recv_sem=proj_recv,
            device_id=(2 * other + core, c), device_id_type=MESH,
        )

    def wait_bytes(ref, sem):
        pltpu.make_async_copy(ref, ref, sem).wait()

    load_vir.wait()
    tail = vir[16:20, :].astype(F32)
    vsend[0:16, :] = vir[0:16, :]
    vsend[16:32, :] = jnp.concatenate([tail, tail, tail, tail], axis=0).astype(BF16)
    coeffs[core, chip, :, :] = vsend[...]
    load_ao.wait()
    turns = []
    for quarter in range(4):
        ahead = (quarter + 4 - z // 2) % 4
        turns.append(jnp.where(ahead == 0, 3, jnp.where(ahead == 1, 1, jnp.where(ahead == 2, 0, 2))))
    for dest in range(PLANE):
        tails = []
        for quarter in range(4):
            panel = 8 * (quarter // 2) + 2 * (dest % 4) + dest // 16
            start = 960 * panel + 256 * ((dest // 4) % 4) + 128 * (quarter % 2)
            if start % 128 == 0:
                tile = ao[:, start : start + 128].astype(F32)
            else:
                after = min(start + 64, 15360 - 128)
                tile = jnp.concatenate([ao[:, start : start + 64], ao[:, after : after + 64]], axis=1).astype(F32)
            stage[dest, pl.ds(pl.multiple_of(16 + 16 * turns[quarter], 16), 16), :] = tile[0:16].astype(BF16)
            tails.append(tile[16:20])
        stage[dest, 0:16, :] = jnp.concatenate(tails, axis=0).astype(BF16)
    raw[place, :, :] = stage[place, :, :]

    pl.semaphore_wait(barrier, PLANE - 1 + LINE - 1 + 7)

    @pl.loop(1, 16)
    def _(step):
        vir_copy((chip + 7 * step) % 16).start()

    for turn in range(len(SPANS)):

        @pl.loop(1, PLANE)
        def _(step):
            raw_copy((place + 7 * step) % PLANE, turn).start()

    wait_bytes(coeffs.at[core, pl.ds(0, 15)], vir_recv)
    pass_copy.start()
    pass_copy.wait_recv()

    coeff = coeffs[:, :, 0:16, :].reshape(512, 128)
    coeff_tail = coeffs[:, :, 16:32, :].reshape(512, 128).astype(F32)
    which = (lax.broadcasted_iota(jnp.int32, (512, 128), 0) // 4) % 4
    for turn in range(4):
        quarter = (z // 2 + SHIFTS[turn]) % 4
        if AWAITS[turn] is not None:
            first, last = SPANS[AWAITS[turn]]
            wait_bytes(raw.at[pl.ds(0, PLANE - 1), first:last], raw_recv.at[AWAITS[turn]])
        ints = raw[:, 16 * turn + 16 : 16 * turn + 32, :].reshape(512, 128)
        ints_tail = raw[:, 0:16, :].reshape(512, 128)
        picked = jnp.where(which == quarter, coeff_tail, 0.0).astype(BF16)
        half = contract_first(ints, coeff) + contract_first(ints_tail, picked)
        for which_half in range(2):
            other = 2 * quarter + which_half
            part[other, :, :] = half[UNIT * which_half : UNIT * (which_half + 1), :]
            if turn < 3:
                term_copy(other).start()
            else:

                @pl.when(other != z)
                def _():
                    term_copy(other).start()

    terms[z, :, :] = part[z, :, :]
    wait_bytes(terms.at[pl.ds(0, LINE - 1)], term_recv)
    total = terms[0, :, :]
    for s in range(1, LINE):
        total = total + terms[s, :, :]
    unit[...] = total.astype(BF16)

    @pl.when(owns)
    def _():
        pltpu.make_async_copy(unit, rowp.at[spot], row_recv.at[y]).start()

        @pl.loop(1, 16)
        def _(step):
            row_copy((c + 7 * step) % 16).start()

    for half in range(2):

        @pl.when(jnp.logical_and(at_home, zh == half))
        def _():
            pltpu.make_async_copy(unit, held.at[zl], hold_recv).start()

        @pl.when(jnp.logical_not(jnp.logical_and(at_home, zh == half)))
        def _():
            hold_copy(half).start()

    @pl.when(holds)
    def _():
        wait_bytes(held, hold_recv)

        @pl.loop(0, 4)
        def _(step):
            other = (x + step) % 4

            @pl.when(col_here(other))
            def _():
                pltpu.make_async_copy(held, colp.at[col_span], col_recv).start()

            @pl.when(jnp.logical_not(col_here(other)))
            def _():
                col_copy(other).start()

    load_naf.wait()
    share = jnp.zeros((naf.shape[0], 128), F32)
    for group in range(4):
        have = slice(4 * group, min(4 * group + 4, PANEL))
        wait_bytes(rowp.at[have], row_recv.at[group])
        rows = rowp[have, :, :].reshape(-1, 128)
        cols = naf[:, UNIT * have.start : UNIT * have.stop]
        share = share + lax.dot_general(cols, rows, (((1,), (0,)), ((), ())), preferred_element_type=F32)
    share = share.T
    for other in range(16):
        proj[other % 2, other // 2, :, :] = share[8 * other : 8 * other + 8, :]
    pair_copy.start()
    pair_copy.wait_recv()
    sums[...] = proj[core] + pair[...]

    @pl.loop(1, 8)
    def _(step):
        proj_copy((4 * zh + x + step) % 8).start()

    projs[4 * zh + x, :, :] = sums[4 * zh + x, :, :]

    wait_bytes(colp.at[half_span], col_recv)
    half_copy.start()
    half_copy.wait_recv()
    cols = colp[0:PANEL, :, :].reshape(PANEL * UNIT, 128)
    for band in range(5):
        block = rowp[3 * band : 3 * band + 3, :, :].reshape(3 * UNIT, 128)
        gram_ref[3 * UNIT * band : 3 * UNIT * (band + 1), :] = contract_second(block, cols) * (1.0 / 128)

    wait_bytes(projs.at[pl.ds(0, 7)], proj_recv)
    total = projs[0, :, :]
    for s in range(1, 8):
        total = total + projs[s, :, :]
    naf_ref[...] = total

    wait_bytes(coeffs.at[core, pl.ds(0, 15)], vir_send)
    pass_copy.wait_send()
    for turn in range(len(SPANS)):
        first, last = SPANS[turn]
        wait_bytes(stage.at[pl.ds(0, PLANE - 1), first:last], raw_send.at[turn])
    wait_bytes(part.at[pl.ds(0, LINE - 1)], term_send)

    @pl.when(owns)
    def _():
        wait_bytes(rowp, row_send)

    for count in range(1, 3):

        @pl.when(jnp.where(at_home, 1, 2) == count)
        def _():
            wait_bytes(held.at[0:count], hold_send)

    for count in range(3, 5):

        @pl.when(jnp.logical_and(holds, jnp.where(col_here(x), 3, 4) == count))
        def _():
            wait_bytes(terms.at[0 : 2 * count], col_send)

    half_copy.wait_send()
    pair_copy.wait_send()
    wait_bytes(sums.at[pl.ds(0, 7)], proj_send)


BANDS = 8


def spill(gram_ref, naf_ref, gram_hbm, naf_hbm, sems):
    rows = gram_ref.shape[0] // BANDS
    copies = [pltpu.make_async_copy(naf_ref, naf_hbm, sems.at[BANDS])]
    for band in range(BANDS):
        span = pl.ds(rows * band, rows)
        copies.append(pltpu.make_async_copy(gram_ref.at[span], gram_hbm.at[span], sems.at[band]))
    for copy in copies:
        copy.start()
    for copy in copies:
        copy.wait()


def shards(ao_ints, vir_coef, naf_vectors):
    dma = pltpu.SemaphoreType.DMA
    hbm = pl.BlockSpec(memory_space=pltpu.HBM)
    gram, naf_ints = pl.pallas_call(
        kernel,
        out_shape=(
            jax.ShapeDtypeStruct((960, 960), F32),
            jax.ShapeDtypeStruct((8, 448), F32),
        ),
        in_specs=[hbm, hbm, hbm],
        out_specs=(
            pl.BlockSpec(memory_space=pltpu.VMEM),
            pl.BlockSpec(memory_space=pltpu.VMEM),
        ),
        scratch_shapes=[
            pltpu.VMEM((20, 15360), BF16),
            pltpu.VMEM((20, 128), BF16),
            pltpu.VMEM((448, 960), BF16),
            pltpu.VMEM((PLANE, 80, 128), BF16),
            pltpu.VMEM((PLANE, 80, 128), BF16),
            pltpu.VMEM((32, 128), BF16),
            pltpu.VMEM((2, 16, 32, 128), BF16),
            pltpu.VMEM((LINE, UNIT, 128), F32),
            pltpu.VMEM((LINE, UNIT, 128), F32),
            pltpu.VMEM((UNIT, 128), BF16),
            pltpu.VMEM((PANEL, UNIT, 128), BF16),
            pltpu.VMEM((4, UNIT, 128), BF16),
            pltpu.VMEM((16, UNIT, 128), BF16),
            pltpu.VMEM((2, 8, 8, 448), F32),
            pltpu.VMEM((8, 8, 448), F32),
            pltpu.VMEM((8, 8, 448), F32),
            pltpu.VMEM((8, 8, 448), F32),
            dma((3,)), dma, dma, dma, dma, dma((3,)), dma((3,)), dma, dma,
            dma, dma((4,)), dma, dma, dma, dma, dma, dma, dma, dma, dma, dma,
        ],
        compiler_params=pltpu.CompilerParams(
            collective_id=0, has_side_effects=True, vmem_limit_bytes=40 * 1024 * 1024
        ),
        name="gram_and_projection",
    )(*(pltpu.with_memory_space_constraint(a, pltpu.HBM) for a in (ao_ints, vir_coef, naf_vectors.T)))
    return pl.pallas_call(
        spill,
        out_shape=(
            jax.ShapeDtypeStruct((960, 960), F32),
            jax.ShapeDtypeStruct((8, 448), F32),
        ),
        in_specs=[pl.BlockSpec(memory_space=pltpu.VMEM)] * 2,
        out_specs=(hbm, hbm),
        scratch_shapes=[dma((BANDS + 1,))],
        compiler_params=pltpu.CompilerParams(vmem_limit_bytes=16 * 1024 * 1024),
        name="spill",
    )(gram, naf_ints)


def solution(mesh):
    in_specs = (P(("row", "col"), None), P(("row", "col"), None), P("row", "col"))
    out_specs = (P("row", "col"), P("row", "col"))
    return jax.shard_map(shards, mesh=mesh, in_specs=in_specs, out_specs=out_specs, check_vma=False)
```

time: 54.9 us -> 50.8 us (0.925)
  local copies, waits for them, and re-layouts: 2.53 us -> 0 us
  Pallas kernels: 51.6 us -> 50.1 us
    pallas_call x1, Pallas kernels: 51.6 us -> 48.1 us  [shards(): pl.pallas_call(kernel, out_shape=(jax.ShapeDtypeStruct((960, 960), F32),...]
    unnamed x2 -> x0, local copies, waits for them, and re-layouts: 2.53 us -> none
    pallas_call x0 -> x1, Pallas kernels: none -> 2 us  [shards(): pl.pallas_call(spill, out_shape=(jax.ShapeDtypeStruct((960, 960), F32), j...]
where the time goes in v3:
time: 50.8 us; the launch traced here: 50.7 us
  Pallas kernels  50.1 us (99%)
  between operations  0.64 us (1%)
    pallas_call x1, Pallas kernels, shards(): pl.pallas_call(kernel, out_shape=(jax.ShapeDtypeStruct((960, 960), F32),...  48.1 us
    pallas_call x1, Pallas kernels, shards(): pl.pallas_call(spill, out_shape=(jax.ShapeDtypeStruct((960, 960), F32), j...  2 us

profile of v3, /device:TPU:1, one launch (start us, length us, event | category | flops | bytes accessed | tf_op | source)
XLA Modules:
  0.0 50.7 jit_solution(6535199330330758520)
XLA Ops:
  0.6 48.1 %gram_and_projection.1 = (f32[960,960]{1,0:T(8,128)S(1)}, f32[8,448]{1,0:T(8,128)S(1)}) custom-call(bf16[20,15360]{1,0:T(8,128)(2,1)} %ao_hbm.1, bf16[20,128]{1,0:T(8,128)(2,1)} %vir_hbm.1, bf16[448,960]{1,0:T(8,128)(2,1)} %bitcast.1), custom_call_target="tpu_custom_call" | custom-call | tf_op jit(solution)/shard_map/gram_and_projection/pallas_call | solution.py:343
  48.7 2.0 %spill.1 = (f32[960,960]{1,0:T(8,128)}, f32[8,448]{1,0:T(8,128)}) custom-call(f32[960,960]{1,0:T(8,128)S(1)} %get-tuple-element.4.gram_ref, f32[8,448]{1,0:T(8,128)S(1)} %get-tuple-element.5.naf_ref), custom_call_target="tpu_custom_call" | custom-call | tf_op jit(solution)/shard_map/spill/pallas_call | solution.py:380

commit v4 on v3

--- a/solution.py
+++ b/solution.py
@@ -14,8 +14,8 @@
 UNIT = 64
 PANEL = 15
 SHIFTS = (2, 1, 3, 0)
-SPANS = ((0, 48), (48, 64), (64, 80))
-AWAITS = (0, None, 1, 2)
+SPANS = ((0, 32), (32, 48), (48, 64), (64, 80))
+FAR_FIRST = (2, 1, 3, 0)
 
 
 def contract_first(lhs, rhs):
@@ -60,17 +60,13 @@
     def in_line(where):
         return 8 * (where // 4) + i, 4 * (where % 4) + y
 
-    @pl.loop(1, PLANE)
-    def _(step):
-        greet(*in_plane((place + step) % PLANE))
-
-    @pl.loop(1, LINE)
-    def _(step):
+    for step in (4, 3, 5, 2, 6, 1, 7):
         greet(*in_line((z + step) % LINE))
-
-    @pl.loop(1, 8)
-    def _(step):
-        greet(8 * (1 - zh) + (i + step) % 8, c)
+    for along in FAR_FIRST:
+        for across in FAR_FIRST:
+            for other in range(2):
+                if along or across or other:
+                    greet(*in_plane(16 * ((core + other) % 2) + 4 * ((y + across) % 4) + (x + along) % 4))
 
     def vir_copy(other):
         return pltpu.make_async_remote_copy(
@@ -138,18 +134,20 @@
         device_id=(r + 1 - 2 * core, c), device_id_type=MESH,
     )
 
-    pair_copy = pltpu.make_async_remote_copy(
-        src_ref=proj.at[1 - core], dst_ref=pair,
-        send_sem=pair_send, recv_sem=pair_recv,
-        device_id=(r + 1 - 2 * core, c), device_id_type=MESH,
-    )
-
-    def proj_copy(other):
-        return pltpu.make_async_remote_copy(
-            src_ref=sums.at[other], dst_ref=projs.at[4 * zh + x],
-            send_sem=proj_send, recv_sem=proj_recv,
-            device_id=(2 * other + core, c), device_id_type=MESH,
-        )
+    def pair_copy(half):
+        return pltpu.make_async_remote_copy(
+            src_ref=proj.at[1 - core, half], dst_ref=pair.at[half],
+            send_sem=pair_send.at[half], recv_sem=pair_recv.at[half],
+            device_id=(r + 1 - 2 * core, c), device_id_type=MESH,
+        )
+
+    def proj_copy(half, other, sent):
+        if sent:
+            pltpu.make_async_remote_copy(
+                src_ref=sums.at[half, other], dst_ref=projs.at[4 * zh + x],
+                send_sem=proj_send, recv_sem=proj_recv,
+                device_id=(8 * half + 2 * other + core, c), device_id_type=MESH,
+            ).start()
 
     def wait_bytes(ref, sem):
         pltpu.make_async_copy(ref, ref, sem).wait()
@@ -179,7 +177,7 @@
         stage[dest, 0:16, :] = jnp.concatenate(tails, axis=0).astype(BF16)
     raw[place, :, :] = stage[place, :, :]
 
-    pl.semaphore_wait(barrier, PLANE - 1 + LINE - 1 + 7)
+    pl.semaphore_wait(barrier, PLANE - 1 + LINE - 1)
 
     @pl.loop(1, 16)
     def _(step):
@@ -187,26 +185,28 @@
 
     for turn in range(len(SPANS)):
 
-        @pl.loop(1, PLANE)
-        def _(step):
-            raw_copy((place + 7 * step) % PLANE, turn).start()
+        for along in FAR_FIRST:
+            for across in FAR_FIRST:
+                for other in range(2):
+                    if along or across or other:
+                        raw_copy(16 * ((core + other) % 2) + 4 * ((y + across) % 4) + (x + along) % 4, turn).start()
 
     wait_bytes(coeffs.at[core, pl.ds(0, 15)], vir_recv)
     pass_copy.start()
     pass_copy.wait_recv()
 
-    coeff = coeffs[:, :, 0:16, :].reshape(512, 128)
-    coeff_tail = coeffs[:, :, 16:32, :].reshape(512, 128).astype(F32)
-    which = (lax.broadcasted_iota(jnp.int32, (512, 128), 0) // 4) % 4
+    coeff = coeffs[:, :, 0:16, :].reshape(512, 128).T
+    coeff_tail = coeffs[:, :, 16:32, :].reshape(512, 128).T.astype(F32)
+    which = (lax.broadcasted_iota(jnp.int32, (128, 512), 1) // 4) % 4
     for turn in range(4):
         quarter = (z // 2 + SHIFTS[turn]) % 4
-        if AWAITS[turn] is not None:
-            first, last = SPANS[AWAITS[turn]]
-            wait_bytes(raw.at[pl.ds(0, PLANE - 1), first:last], raw_recv.at[AWAITS[turn]])
+        first, last = SPANS[turn]
+        wait_bytes(raw.at[pl.ds(0, PLANE - 1), first:last], raw_recv.at[turn])
         ints = raw[:, 16 * turn + 16 : 16 * turn + 32, :].reshape(512, 128)
         ints_tail = raw[:, 0:16, :].reshape(512, 128)
         picked = jnp.where(which == quarter, coeff_tail, 0.0).astype(BF16)
-        half = contract_first(ints, coeff) + contract_first(ints_tail, picked)
+        half = jnp.dot(coeff, ints, preferred_element_type=F32) + jnp.dot(picked, ints_tail, preferred_element_type=F32)
+        half = half.T
         for which_half in range(2):
             other = 2 * quarter + which_half
             part[other, :, :] = half[UNIT * which_half : UNIT * (which_half + 1), :]
@@ -229,9 +229,10 @@
     def _():
         pltpu.make_async_copy(unit, rowp.at[spot], row_recv.at[y]).start()
 
-        @pl.loop(1, 16)
-        def _(step):
-            row_copy((c + 7 * step) % 16).start()
+        for along in FAR_FIRST:
+            for across in FAR_FIRST:
+                if along or across:
+                    row_copy(4 * ((zl + along) % 4) + (y + across) % 4).start()
 
     for half in range(2):
 
@@ -260,25 +261,21 @@
                 col_copy(other).start()
 
     load_naf.wait()
-    share = jnp.zeros((naf.shape[0], 128), F32)
     for group in range(4):
         have = slice(4 * group, min(4 * group + 4, PANEL))
         wait_bytes(rowp.at[have], row_recv.at[group])
-        rows = rowp[have, :, :].reshape(-1, 128)
-        cols = naf[:, UNIT * have.start : UNIT * have.stop]
-        share = share + lax.dot_general(cols, rows, (((1,), (0,)), ((), ())), preferred_element_type=F32)
-    share = share.T
+    rows = rowp[...].reshape(PANEL * UNIT, 128)
+    share = lax.dot_general(rows, naf[...], (((0,), (1,)), ((), ())), preferred_element_type=F32)
     for other in range(16):
-        proj[other % 2, other // 2, :, :] = share[8 * other : 8 * other + 8, :]
-    pair_copy.start()
-    pair_copy.wait_recv()
-    sums[...] = proj[core] + pair[...]
-
-    @pl.loop(1, 8)
-    def _(step):
-        proj_copy((4 * zh + x + step) % 8).start()
-
-    projs[4 * zh + x, :, :] = sums[4 * zh + x, :, :]
+        proj[other % 2, other // 8, (other // 2) % 4, :, :] = share[8 * other : 8 * other + 8, :]
+    pair_copy(1 - zh).start()
+    pair_copy(zh).start()
+    for half in (1 - zh, zh):
+        pair_copy(half).wait_recv()
+        sums[half, :, :, :] = proj[core, half] + pair[half]
+        for step in FAR_FIRST:
+            proj_copy(half, (x + step) % 4, half is not zh or step != 0)
+    projs[4 * zh + x, :, :] = sums[zh, x]
 
     wait_bytes(colp.at[half_span], col_recv)
     half_copy.start()
@@ -288,12 +285,6 @@
         block = rowp[3 * band : 3 * band + 3, :, :].reshape(3 * UNIT, 128)
         gram_ref[3 * UNIT * band : 3 * UNIT * (band + 1), :] = contract_second(block, cols) * (1.0 / 128)
 
-    wait_bytes(projs.at[pl.ds(0, 7)], proj_recv)
-    total = projs[0, :, :]
-    for s in range(1, 8):
-        total = total + projs[s, :, :]
-    naf_ref[...] = total
-
     wait_bytes(coeffs.at[core, pl.ds(0, 15)], vir_send)
     pass_copy.wait_send()
     for turn in range(len(SPANS)):
@@ -318,8 +309,15 @@
             wait_bytes(terms.at[0 : 2 * count], col_send)
 
     half_copy.wait_send()
-    pair_copy.wait_send()
-    wait_bytes(sums.at[pl.ds(0, 7)], proj_send)
+    for half in range(2):
+        pair_copy(half).wait_send()
+    wait_bytes(projs.at[pl.ds(0, 7)], proj_recv)
+    total = projs[0, :, :]
+    for s in range(1, 8):
+        total = total + projs[s, :, :]
+    naf_ref[...] = total
+
+    wait_bytes(projs.at[pl.ds(0, 7)], proj_send)
 
 
 BANDS = 8
@@ -365,12 +363,12 @@
             pltpu.VMEM((PANEL, UNIT, 128), BF16),
             pltpu.VMEM((4, UNIT, 128), BF16),
             pltpu.VMEM((16, UNIT, 128), BF16),
-            pltpu.VMEM((2, 8, 8, 448), F32),
+            pltpu.VMEM((2, 2, 4, 8, 448), F32),
+            pltpu.VMEM((2, 4, 8, 448), F32),
+            pltpu.VMEM((2, 4, 8, 448), F32),
             pltpu.VMEM((8, 8, 448), F32),
-            pltpu.VMEM((8, 8, 448), F32),
-            pltpu.VMEM((8, 8, 448), F32),
-            dma((3,)), dma, dma, dma, dma, dma((3,)), dma((3,)), dma, dma,
-            dma, dma((4,)), dma, dma, dma, dma, dma, dma, dma, dma, dma, dma,
+            dma((3,)), dma, dma, dma, dma, dma((4,)), dma((4,)), dma, dma,
+            dma, dma((4,)), dma, dma, dma, dma, dma, dma, dma((2,)), dma((2,)), dma, dma,
         ],
         compiler_params=pltpu.CompilerParams(
             collective_id=0, has_side_effects=True, vmem_limit_bytes=40 * 1024 * 1024

time: 50.8 us -> 47.4 us (0.933)
  Pallas kernels: 50.1 us -> 46.7 us
    pallas_call x1, Pallas kernels: 48.1 us -> 44.7 us  [shards(): pl.pallas_call(kernel, out_shape=(jax.ShapeDtypeStruct((960, 960), F32),...]
where the time goes in v4:
time: 47.4 us; the launch traced here: 47.3 us
  Pallas kernels  46.7 us (99%)
  between operations  0.64 us (1%)
    pallas_call x1, Pallas kernels, shards(): pl.pallas_call(kernel, out_shape=(jax.ShapeDtypeStruct((960, 960), F32),...  44.7 us
    pallas_call x1, Pallas kernels, shards(): pl.pallas_call(spill, out_shape=(jax.ShapeDtypeStruct((960, 960), F32), j...  2 us

profile of v4, /device:TPU:1, one launch (start us, length us, event | category | flops | bytes accessed | tf_op | source)
XLA Modules:
  0.0 47.3 jit_solution(8748851750553810020)
XLA Ops:
  0.6 44.7 %gram_and_projection.1 = (f32[960,960]{1,0:T(8,128)S(1)}, f32[8,448]{1,0:T(8,128)S(1)}) custom-call(bf16[20,15360]{1,0:T(8,128)(2,1)} %ao_hbm.1, bf16[20,128]{1,0:T(8,128)(2,1)} %vir_hbm.1, bf16[448,960]{1,0:T(8,128)(2,1)} %bitcast.1), custom_call_target="tpu_custom_call" | custom-call | tf_op jit(solution)/shard_map/gram_and_projection/pallas_call | solution.py:341
  45.3 2.0 %spill.1 = (f32[960,960]{1,0:T(8,128)}, f32[8,448]{1,0:T(8,128)}) custom-call(f32[960,960]{1,0:T(8,128)S(1)} %get-tuple-element.4.gram_ref, f32[8,448]{1,0:T(8,128)S(1)} %get-tuple-element.5.naf_ref), custom_call_target="tpu_custom_call" | custom-call | tf_op jit(solution)/shard_map/spill/pallas_call | solution.py:378

commit v5 on v4

--- a/solution.py
+++ b/solution.py
@@ -30,7 +30,7 @@
     ao_hbm, vir_hbm, naf_hbm, gram_ref, naf_ref,
     ao, vir, naf, stage, raw, vsend, coeffs, part, terms, unit, rowp, held, colp, proj, pair, sums, projs,
     load_sem, vir_send, vir_recv, pass_send, pass_recv, raw_send, raw_recv, term_send, term_recv,
-    row_send, row_recv, hold_send, hold_recv, col_send, col_recv, half_send, half_recv, pair_send, pair_recv, proj_send, proj_recv,
+    row_send, row_recv, hold_send, hold_recv, col_send, col_recv, half_send, half_recv, pair_send, pair_recv, proj_send, proj_recv, meet,
 ):
     r = lax.axis_index("row")
     c = lax.axis_index("col")
@@ -45,9 +45,6 @@
     load_ao = pltpu.make_async_copy(ao_hbm, ao, load_sem.at[0])
     load_naf = pltpu.make_async_copy(naf_hbm, naf, load_sem.at[1])
     load_vir = pltpu.make_async_copy(vir_hbm, vir, load_sem.at[2])
-    load_vir.start()
-    load_ao.start()
-    load_naf.start()
 
     barrier = pltpu.get_barrier_semaphore()
 
@@ -60,13 +57,16 @@
     def in_line(where):
         return 8 * (where // 4) + i, 4 * (where % 4) + y
 
-    for step in (4, 3, 5, 2, 6, 1, 7):
+    for step in (1, 7):
         greet(*in_line((z + step) % LINE))
     for along in FAR_FIRST:
         for across in FAR_FIRST:
             for other in range(2):
                 if along or across or other:
                     greet(*in_plane(16 * ((core + other) % 2) + 4 * ((y + across) % 4) + (x + along) % 4))
+    load_vir.start()
+    load_ao.start()
+    load_naf.start()
 
     def vir_copy(other):
         return pltpu.make_async_remote_copy(
@@ -177,7 +177,13 @@
         stage[dest, 0:16, :] = jnp.concatenate(tails, axis=0).astype(BF16)
     raw[place, :, :] = stage[place, :, :]
 
-    pl.semaphore_wait(barrier, PLANE - 1 + LINE - 1)
+    pl.semaphore_wait(barrier, PLANE - 1 + 2)
+
+    def tell(turn, step):
+        pl.semaphore_signal(meet.at[turn], inc=1, device_id=in_line((z + step) % LINE), device_id_type=MESH)
+
+    tell(0, 1)
+    tell(0, 7)
 
     @pl.loop(1, 16)
     def _(step):
@@ -191,8 +197,12 @@
                     if along or across or other:
                         raw_copy(16 * ((core + other) % 2) + 4 * ((y + across) % 4) + (x + along) % 4, turn).start()
 
+    pl.semaphore_wait(meet.at[0], 2)
+    tell(1, 2)
+    tell(1, 6)
     wait_bytes(coeffs.at[core, pl.ds(0, 15)], vir_recv)
     pass_copy.start()
+    pl.semaphore_wait(meet.at[1], 2)
     pass_copy.wait_recv()
 
     coeff = coeffs[:, :, 0:16, :].reshape(512, 128).T
@@ -244,22 +254,6 @@
         def _():
             hold_copy(half).start()
 
-    @pl.when(holds)
-    def _():
-        wait_bytes(held, hold_recv)
-
-        @pl.loop(0, 4)
-        def _(step):
-            other = (x + step) % 4
-
-            @pl.when(col_here(other))
-            def _():
-                pltpu.make_async_copy(held, colp.at[col_span], col_recv).start()
-
-            @pl.when(jnp.logical_not(col_here(other)))
-            def _():
-                col_copy(other).start()
-
     load_naf.wait()
     for group in range(4):
         have = slice(4 * group, min(4 * group + 4, PANEL))
@@ -270,6 +264,22 @@
         proj[other % 2, other // 8, (other // 2) % 4, :, :] = share[8 * other : 8 * other + 8, :]
     pair_copy(1 - zh).start()
     pair_copy(zh).start()
+    @pl.when(holds)
+    def _():
+        wait_bytes(held, hold_recv)
+
+        @pl.loop(0, 4)
+        def _(step):
+            other = (x + step) % 4
+
+            @pl.when(col_here(other))
+            def _():
+                pltpu.make_async_copy(held, colp.at[col_span], col_recv).start()
+
+            @pl.when(jnp.logical_not(col_here(other)))
+            def _():
+                col_copy(other).start()
+
     for half in (1 - zh, zh):
         pair_copy(half).wait_recv()
         sums[half, :, :, :] = proj[core, half] + pair[half]
@@ -369,6 +379,7 @@
             pltpu.VMEM((8, 8, 448), F32),
             dma((3,)), dma, dma, dma, dma, dma((4,)), dma((4,)), dma, dma,
             dma, dma((4,)), dma, dma, dma, dma, dma, dma, dma((2,)), dma((2,)), dma, dma,
+            pltpu.SemaphoreType.REGULAR((2,)),
         ],
         compiler_params=pltpu.CompilerParams(
             collective_id=0, has_side_effects=True, vmem_limit_bytes=40 * 1024 * 1024

time: 47.4 us -> 44.8 us (0.945)
  Pallas kernels: 46.7 us -> 43.7 us
    pallas_call x1, Pallas kernels: 44.7 us -> 41.7 us  [shards(): pl.pallas_call(kernel, out_shape=(jax.ShapeDtypeStruct((960, 960), F32),...]
where the time goes in v5:
time: 44.8 us; the launch traced here: 44.3 us
  Pallas kernels  43.7 us (98%)
  between operations  0.64 us (1%)
    pallas_call x1, Pallas kernels, shards(): pl.pallas_call(kernel, out_shape=(jax.ShapeDtypeStruct((960, 960), F32),...  41.7 us
    pallas_call x1, Pallas kernels, shards(): pl.pallas_call(spill, out_shape=(jax.ShapeDtypeStruct((960, 960), F32), j...  2 us

profile of v5, /device:TPU:1, one launch (start us, length us, event | category | flops | bytes accessed | tf_op | source)
XLA Modules:
  0.0 44.3 jit_solution(9421575309858213167)
XLA Ops:
  0.6 41.7 %gram_and_projection.1 = (f32[960,960]{1,0:T(8,128)S(1)}, f32[8,448]{1,0:T(8,128)S(1)}) custom-call(bf16[20,15360]{1,0:T(8,128)(2,1)} %ao_hbm.1, bf16[20,128]{1,0:T(8,128)(2,1)} %vir_hbm.1, bf16[448,960]{1,0:T(8,128)(2,1)} %bitcast.1), custom_call_target="tpu_custom_call" | custom-call | tf_op jit(solution)/shard_map/gram_and_projection/pallas_call | solution.py:351
  42.3 2.0 %spill.1 = (f32[960,960]{1,0:T(8,128)}, f32[8,448]{1,0:T(8,128)}) custom-call(f32[960,960]{1,0:T(8,128)S(1)} %get-tuple-element.4.gram_ref, f32[8,448]{1,0:T(8,128)S(1)} %get-tuple-element.5.naf_ref), custom_call_target="tpu_custom_call" | custom-call | tf_op jit(solution)/shard_map/spill/pallas_call | solution.py:389

commit v6 on v5

--- a/solution.py
+++ b/solution.py
@@ -27,8 +27,8 @@
 
 
 def kernel(
-    ao_hbm, vir_hbm, naf_hbm, gram_ref, naf_ref,
-    ao, vir, naf, stage, raw, vsend, coeffs, part, terms, unit, rowp, held, colp, proj, pair, sums, projs,
+    ao_hbm, vir_hbm, naf_hbm, rowp, colp, naf_ref,
+    ao, vir, naf, stage, raw, vsend, coeffs, part, terms, unit, held, proj, pair, sums, projs,
     load_sem, vir_send, vir_recv, pass_send, pass_recv, raw_send, raw_recv, term_send, term_recv,
     row_send, row_recv, hold_send, hold_recv, col_send, col_recv, half_send, half_recv, pair_send, pair_recv, proj_send, proj_recv, meet,
 ):
@@ -155,7 +155,7 @@
     load_vir.wait()
     tail = vir[16:20, :].astype(F32)
     vsend[0:16, :] = vir[0:16, :]
-    vsend[16:32, :] = jnp.concatenate([tail, tail, tail, tail], axis=0).astype(BF16)
+    vsend[16:24, :] = jnp.concatenate([tail, tail], axis=0).astype(BF16)
     coeffs[core, chip, :, :] = vsend[...]
     load_ao.wait()
     turns = []
@@ -185,9 +185,10 @@
     tell(0, 1)
     tell(0, 7)
 
-    @pl.loop(1, 16)
-    def _(step):
-        vir_copy((chip + 7 * step) % 16).start()
+    for along in FAR_FIRST:
+        for across in FAR_FIRST:
+            if along or across:
+                vir_copy(4 * ((y + across) % 4) + (x + along) % 4).start()
 
     for turn in range(len(SPANS)):
 
@@ -206,7 +207,8 @@
     pass_copy.wait_recv()
 
     coeff = coeffs[:, :, 0:16, :].reshape(512, 128).T
-    coeff_tail = coeffs[:, :, 16:32, :].reshape(512, 128).T.astype(F32)
+    coeff_tail = coeffs[:, :, 16:24, :].astype(F32)
+    coeff_tail = jnp.concatenate([coeff_tail, coeff_tail], axis=2).reshape(512, 128).T
     which = (lax.broadcasted_iota(jnp.int32, (128, 512), 1) // 4) % 4
     for turn in range(4):
         quarter = (z // 2 + SHIFTS[turn]) % 4
@@ -270,7 +272,7 @@
 
         @pl.loop(0, 4)
         def _(step):
-            other = (x + step) % 4
+            other = (x + 2 + 3 * step) % 4
 
             @pl.when(col_here(other))
             def _():
@@ -290,11 +292,6 @@
     wait_bytes(colp.at[half_span], col_recv)
     half_copy.start()
     half_copy.wait_recv()
-    cols = colp[0:PANEL, :, :].reshape(PANEL * UNIT, 128)
-    for band in range(5):
-        block = rowp[3 * band : 3 * band + 3, :, :].reshape(3 * UNIT, 128)
-        gram_ref[3 * UNIT * band : 3 * UNIT * (band + 1), :] = contract_second(block, cols) * (1.0 / 128)
-
     wait_bytes(coeffs.at[core, pl.ds(0, 15)], vir_send)
     pass_copy.wait_send()
     for turn in range(len(SPANS)):
@@ -330,49 +327,49 @@
     wait_bytes(projs.at[pl.ds(0, 7)], proj_send)
 
 
-BANDS = 8
-
-
-def spill(gram_ref, naf_ref, gram_hbm, naf_hbm, sems):
-    rows = gram_ref.shape[0] // BANDS
-    copies = [pltpu.make_async_copy(naf_ref, naf_hbm, sems.at[BANDS])]
+BANDS = 5
+
+
+def finish(rowp, colp, naf_ref, gram_hbm, naf_hbm, gram, sems):
+    pltpu.make_async_copy(naf_ref, naf_hbm, sems.at[BANDS]).start()
+    cols = colp[0:PANEL, :, :].reshape(PANEL * UNIT, 128)
+    rows = PANEL * UNIT // BANDS
+    copies = []
     for band in range(BANDS):
+        block = rowp[3 * band : 3 * band + 3, :, :].reshape(rows, 128)
+        gram[rows * band : rows * (band + 1), :] = contract_second(block, cols) * (1.0 / 128)
         span = pl.ds(rows * band, rows)
-        copies.append(pltpu.make_async_copy(gram_ref.at[span], gram_hbm.at[span], sems.at[band]))
-    for copy in copies:
-        copy.start()
+        copies.append(pltpu.make_async_copy(gram.at[span], gram_hbm.at[span], sems.at[band]))
+        copies[-1].start()
     for copy in copies:
         copy.wait()
+    pltpu.make_async_copy(naf_ref, naf_hbm, sems.at[BANDS]).wait()
 
 
 def shards(ao_ints, vir_coef, naf_vectors):
     dma = pltpu.SemaphoreType.DMA
     hbm = pl.BlockSpec(memory_space=pltpu.HBM)
-    gram, naf_ints = pl.pallas_call(
+    rowp, colp, naf_ints = pl.pallas_call(
         kernel,
         out_shape=(
-            jax.ShapeDtypeStruct((960, 960), F32),
+            jax.ShapeDtypeStruct((PANEL, UNIT, 128), BF16),
+            jax.ShapeDtypeStruct((16, UNIT, 128), BF16),
             jax.ShapeDtypeStruct((8, 448), F32),
         ),
         in_specs=[hbm, hbm, hbm],
-        out_specs=(
-            pl.BlockSpec(memory_space=pltpu.VMEM),
-            pl.BlockSpec(memory_space=pltpu.VMEM),
-        ),
+        out_specs=[pl.BlockSpec(memory_space=pltpu.VMEM)] * 3,
         scratch_shapes=[
             pltpu.VMEM((20, 15360), BF16),
             pltpu.VMEM((20, 128), BF16),
             pltpu.VMEM((448, 960), BF16),
             pltpu.VMEM((PLANE, 80, 128), BF16),
             pltpu.VMEM((PLANE, 80, 128), BF16),
-            pltpu.VMEM((32, 128), BF16),
-            pltpu.VMEM((2, 16, 32, 128), BF16),
+            pltpu.VMEM((24, 128), BF16),
+            pltpu.VMEM((2, 16, 24, 128), BF16),
             pltpu.VMEM((LINE, UNIT, 128), F32),
             pltpu.VMEM((LINE, UNIT, 128), F32),
             pltpu.VMEM((UNIT, 128), BF16),
-            pltpu.VMEM((PANEL, UNIT, 128), BF16),
             pltpu.VMEM((4, UNIT, 128), BF16),
-            pltpu.VMEM((16, UNIT, 128), BF16),
             pltpu.VMEM((2, 2, 4, 8, 448), F32),
             pltpu.VMEM((2, 4, 8, 448), F32),
             pltpu.VMEM((2, 4, 8, 448), F32),
@@ -384,20 +381,20 @@
         compiler_params=pltpu.CompilerParams(
             collective_id=0, has_side_effects=True, vmem_limit_bytes=40 * 1024 * 1024
         ),
-        name="gram_and_projection",
+        name="panels_and_projection",
     )(*(pltpu.with_memory_space_constraint(a, pltpu.HBM) for a in (ao_ints, vir_coef, naf_vectors.T)))
     return pl.pallas_call(
-        spill,
+        finish,
         out_shape=(
             jax.ShapeDtypeStruct((960, 960), F32),
             jax.ShapeDtypeStruct((8, 448), F32),
         ),
-        in_specs=[pl.BlockSpec(memory_space=pltpu.VMEM)] * 2,
+        in_specs=[pl.BlockSpec(memory_space=pltpu.VMEM)] * 3,
         out_specs=(hbm, hbm),
-        scratch_shapes=[dma((BANDS + 1,))],
+        scratch_shapes=[pltpu.VMEM((960, 960), F32), dma((BANDS + 1,))],
         compiler_params=pltpu.CompilerParams(vmem_limit_bytes=16 * 1024 * 1024),
-        name="spill",
-    )(gram, naf_ints)
+        name="gram",
+    )(rowp, colp, naf_ints)
 
 
 def solution(mesh):

time: 44.8 us -> 44.2 us (0.987)
  no operation moved by 1% of the time
where the time goes in v6:
time: 44.2 us; the launch traced here: 44 us
  Pallas kernels  43.4 us (98%)
  between operations  0.64 us (1%)
    pallas_call x1, Pallas kernels, shards(): pl.pallas_call(kernel, out_shape=(jax.ShapeDtypeStruct((PANEL, UNIT, 128)...  41.2 us
    pallas_call x1, Pallas kernels, shards(): pl.pallas_call(finish, out_shape=(jax.ShapeDtypeStruct((960, 960), F32),...  2.24 us

profile of v6, /device:TPU:1, one launch (start us, length us, event | category | flops | bytes accessed | tf_op | source)
XLA Modules:
  0.0 44.0 jit_solution(11894685466578965597)
XLA Ops:
  0.6 41.2 %panels_and_projection.1 = (bf16[15,64,128]{2,1,0:T(8,128)(2,1)S(1)}, bf16[16,64,128]{2,1,0:T(8,128)(2,1)S(1)}, f32[8,448]{1,0:T(8,128)S(1)}) custom-call(bf16[20,15360]{1,0:T(8,128)(2,1)} %ao_hbm.1, bf16[20,128]{1,0:T(8,128)(2,1)} %vir_hbm.1, bf16[448,960]{1,0:T(8,128)(2,1)} %bitcast.1), custom_call_target="tpu_custom_call" | custom-call | tf_op jit(solution)/shard_map/panels_and_projection/pallas_call | solution.py:352
  41.8 2.2 %gram.1 = (f32[960,960]{1,0:T(8,128)}, f32[8,448]{1,0:T(8,128)}) custom-call(bf16[15,64,128]{2,1,0:T(8,128)(2,1)S(1)} %get-tuple-element.5.rowp, bf16[16,64,128]{2,1,0:T(8,128)(2,1)S(1)} %get-tuple-element.6.colp, f32[8,448]{1,0:T(8,128)S(1)} %get-tuple-element.7.naf_ref), custom_call_target="tpu_custom_call" | custom-call | tf_op jit(solution)/shard_map/gram/pallas_call | solution.py:386

commit v7 on v6

--- a/solution.py
+++ b/solution.py
@@ -203,7 +203,6 @@
     tell(1, 6)
     wait_bytes(coeffs.at[core, pl.ds(0, 15)], vir_recv)
     pass_copy.start()
-    pl.semaphore_wait(meet.at[1], 2)
     pass_copy.wait_recv()
 
     coeff = coeffs[:, :, 0:16, :].reshape(512, 128).T
@@ -219,6 +218,8 @@
         picked = jnp.where(which == quarter, coeff_tail, 0.0).astype(BF16)
         half = jnp.dot(coeff, ints, preferred_element_type=F32) + jnp.dot(picked, ints_tail, preferred_element_type=F32)
         half = half.T
+        if turn == 0:
+            pl.semaphore_wait(meet.at[1], 2)
         for which_half in range(2):
             other = 2 * quarter + which_half
             part[other, :, :] = half[UNIT * which_half : UNIT * (which_half + 1), :]

time: 44.2 us -> 44.2 us (level)
  no operation moved by 1% of the time
where the time goes in v7:
time: 44.2 us; the launch traced here: 44.1 us
  Pallas kernels  43.4 us (98%)
  between operations  0.64 us (1%)
    pallas_call x1, Pallas kernels, shards(): pl.pallas_call(kernel, out_shape=(jax.ShapeDtypeStruct((PANEL, UNIT, 128)...  41.2 us
    pallas_call x1, Pallas kernels, shards(): pl.pallas_call(finish, out_shape=(jax.ShapeDtypeStruct((960, 960), F32),...  2.24 us

profile of v7, /device:TPU:1, one launch (start us, length us, event | category | flops | bytes accessed | tf_op | source)
XLA Modules:
  0.0 44.1 jit_solution(5817294784965180652)
XLA Ops:
  0.6 41.2 %panels_and_projection.1 = (bf16[15,64,128]{2,1,0:T(8,128)(2,1)S(1)}, bf16[16,64,128]{2,1,0:T(8,128)(2,1)S(1)}, f32[8,448]{1,0:T(8,128)S(1)}) custom-call(bf16[20,15360]{1,0:T(8,128)(2,1)} %ao_hbm.1, bf16[20,128]{1,0:T(8,128)(2,1)} %vir_hbm.1, bf16[448,960]{1,0:T(8,128)(2,1)} %bitcast.1), custom_call_target="tpu_custom_call" | custom-call | tf_op jit(solution)/shard_map/panels_and_projection/pallas_call | solution.py:353
  41.8 2.2 %gram.1 = (f32[960,960]{1,0:T(8,128)}, f32[8,448]{1,0:T(8,128)}) custom-call(bf16[15,64,128]{2,1,0:T(8,128)(2,1)S(1)} %get-tuple-element.5.rowp, bf16[16,64,128]{2,1,0:T(8,128)(2,1)S(1)} %get-tuple-element.6.colp, f32[8,448]{1,0:T(8,128)S(1)} %get-tuple-element.7.naf_ref), custom_call_target="tpu_custom_call" | custom-call | tf_op jit(solution)/shard_map/gram/pallas_call | solution.py:387

commit v8 on v7

--- a/solution.py
+++ b/solution.py
@@ -242,8 +242,8 @@
     def _():
         pltpu.make_async_copy(unit, rowp.at[spot], row_recv.at[y]).start()
 
-        for along in FAR_FIRST:
-            for across in FAR_FIRST:
+        for across in FAR_FIRST:
+            for along in FAR_FIRST:
                 if along or across:
                     row_copy(4 * ((zl + along) % 4) + (y + across) % 4).start()
 

time: 44.2 us -> 45.1 us (1.020)
  Pallas kernels: 43.4 us -> 44.4 us
    pallas_call x1, Pallas kernels: 41.2 us -> 42.1 us  [shards(): pl.pallas_call(kernel, out_shape=(jax.ShapeDtypeStruct((PANEL, UNIT, 128)...]
where the time goes in v8:
time: 45.1 us; the launch traced here: 45 us
  Pallas kernels  44.4 us (98%)
  between operations  0.64 us (1%)
    pallas_call x1, Pallas kernels, shards(): pl.pallas_call(kernel, out_shape=(jax.ShapeDtypeStruct((PANEL, UNIT, 128)...  42.1 us
    pallas_call x1, Pallas kernels, shards(): pl.pallas_call(finish, out_shape=(jax.ShapeDtypeStruct((960, 960), F32),...  2.24 us

profile of v8, /device:TPU:1, one launch (start us, length us, event | category | flops | bytes accessed | tf_op | source)
XLA Modules:
  0.0 45.0 jit_solution(13827407243386062215)
XLA Ops:
  0.6 42.1 %panels_and_projection.1 = (bf16[15,64,128]{2,1,0:T(8,128)(2,1)S(1)}, bf16[16,64,128]{2,1,0:T(8,128)(2,1)S(1)}, f32[8,448]{1,0:T(8,128)S(1)}) custom-call(bf16[20,15360]{1,0:T(8,128)(2,1)} %ao_hbm.1, bf16[20,128]{1,0:T(8,128)(2,1)} %vir_hbm.1, bf16[448,960]{1,0:T(8,128)(2,1)} %bitcast.1), custom_call_target="tpu_custom_call" | custom-call | tf_op jit(solution)/shard_map/panels_and_projection/pallas_call | solution.py:353
  42.8 2.2 %gram.1 = (f32[960,960]{1,0:T(8,128)}, f32[8,448]{1,0:T(8,128)}) custom-call(bf16[15,64,128]{2,1,0:T(8,128)(2,1)S(1)} %get-tuple-element.5.rowp, bf16[16,64,128]{2,1,0:T(8,128)(2,1)S(1)} %get-tuple-element.6.colp, f32[8,448]{1,0:T(8,128)S(1)} %get-tuple-element.7.naf_ref), custom_call_target="tpu_custom_call" | custom-call | tf_op jit(solution)/shard_map/gram/pallas_call | solution.py:387
